TPU v7x, 32 devices: a whole 2x2x4 slice. The times are simulated.
32 devices in a mesh: dp: 4 (over y, core), ctx: 4 (over z), tp: 2 (over x).
Axes of the slice: x: 2, y: 2, z: 4, core: 2. Of those that a mesh axis runs over, the one named last changes fastest.
Arguments:
- tokens: bfloat16 [8, 640, 512], P('dp', 'ctx'), may hold values from -6 to 6
- cotangent: bfloat16 [8, 640, 512], P('dp', 'ctx'), may hold values from -6 to 6
- routes: int32 [8, 640, 2], P('dp', 'ctx'), may hold values from 0 to 15, as said below
- slot_index: int32 [8, 640, 2], P('dp', 'ctx'), may hold values from 0 to 30, as said below
- token_mask: int32 [8, 640], P('dp', 'ctx'), may hold values from 0 to 1, as said below
- image_mask: int32 [8], P('dp'), may hold values from 0 to 1, as said below
- adapter_set: int32 [8], P('dp'), may hold values from 0 to 3
- first_gain: float32 [512], replicated, may hold values from 0.5 to 1.5
- first_shift: float32 [512], replicated, may hold values from -0.5 to 0.5
- second_gain: float32 [512], replicated, may hold values from 0.5 to 1.5
- second_shift: float32 [512], replicated, may hold values from -0.5 to 0.5
- attend_weight: bfloat16 [512, 3, 512], P('dp', None, 'tp'), may hold values from -0.25 to 0.25
- mixing_weight: bfloat16 [512, 512], P('dp', 'tp'), may hold values from -0.75 to 0.75
- router_weight: bfloat16 [512, 16], P('dp'), may hold values from -0.1875 to 0.1875
- expand_weight: bfloat16 [16, 512, 2048], P('dp', None, 'tp'), may hold values from -0.25 to 0.25
- shrink_weight: bfloat16 [16, 2048, 512], P('dp', 'tp'), may hold values from -2 to 2
- attend_down: bfloat16 [4, 512, 16], replicated, may hold values from -0.25 to 0.25
- attend_up: bfloat16 [4, 16, 3, 512], replicated, may hold values from -0.75 to 0.75
- mixing_down: bfloat16 [4, 512, 16], replicated, may hold values from -0.25 to 0.25
- mixing_up: bfloat16 [4, 16, 512], replicated, may hold values from -1.5 to 1.5
- router_down: bfloat16 [4, 512, 16], replicated, may hold values from -0.25 to 0.25
- router_up: bfloat16 [4, 16, 16], replicated, may hold values from -0.75 to 0.75
- expand_down: bfloat16 [4, 16, 512, 16], replicated, may hold values from -0.25 to 0.25
- expand_up: bfloat16 [4, 16, 16, 2048], replicated, may hold values from -0.75 to 0.75
- shrink_down: bfloat16 [4, 16, 2048, 16], replicated, may hold values from -0.125 to 0.125
- shrink_up: bfloat16 [4, 16, 16, 512], replicated, may hold values from -6 to 6
Outputs:
- layer_out: bfloat16 [8, 640, 512], P('dp', 'ctx')
- tokens_grad: bfloat16 [8, 640, 512], P('dp', 'ctx')
- grad_attend_down: float32 [4, 512, 16], replicated
- grad_attend_up: float32 [4, 16, 3, 512], replicated
- grad_mixing_down: float32 [4, 512, 16], replicated
- grad_mixing_up: float32 [4, 16, 512], replicated
- grad_router_down: float32 [4, 512, 16], replicated
- grad_router_up: float32 [4, 16, 16], replicated
- grad_expand_down: float32 [4, 16, 512, 16], replicated
- grad_expand_up: float32 [4, 16, 16, 2048], replicated
- grad_shrink_down: float32 [4, 16, 2048, 16], replicated
- grad_shrink_up: float32 [4, 16, 16, 512], replicated
Inputs may be any that keep to these rules, and one draw needn't show every extreme that they name: `routes`: each token names two different experts. In every image block of 160 positions the first 31 tokens name one common expert first. `slot_index`: A pair's value is the number of earlier pairs (positions in order, a token's first expert before its second) of the same image block that name the same expert and belong to live tokens; pairs of tokens that are not live and pairs counted 30 or more hold 30, which means dropped. `token_mask`: the real tokens of each image are a prefix of more than half of its 640 positions. `image_mask`: the first image is real, and at least one image is a pad.
All inputs are finite; a program needn't handle non-finite values.
Results may differ from a plain program's by a relative error of at most 0.022.
Values may be sent and summed in bfloat16 or wider, within the bound.
A program may use at most 192 MiB of HBM per device.

v0:
```python
import functools

import jax
import jax.numpy as jnp
from jax import lax
from jax.experimental import pallas as pl
from jax.experimental.pallas import tpu as pltpu
from jax.sharding import PartitionSpec as P

D = 512
HEADS = 8
HD = 64
FF = 2048
EXPERTS = 16
TOP = 2
RANK = 16
SETS = 4
CAP = 30
SLOTS = 32
WIDTH = SETS * RANK

EPSILON = 1e-06
MASKED = -1e30
SQRT_HALF = 0.7071067811865476
INV_ROOT_TWO_PI = 0.3989422804014327
F32 = jnp.float32
BF16 = jnp.bfloat16
MESH = pl.DeviceIdType.MESH
ANY = pl.BlockSpec(memory_space=pl.ANY)
IN_VMEM = pl.BlockSpec(memory_space=pltpu.VMEM)


def matmul(left_side, right_side):
    return jnp.dot(left_side, right_side, preferred_element_type=F32)


def inner_rows(left_side, right_side):
    return lax.dot_general(
        left_side, right_side, (((0,), (0,)), ((), ())), preferred_element_type=F32
    )


def times_transposed(left_side, right_side):
    return lax.dot_general(
        left_side, right_side, (((1,), (1,)), ((), ())), preferred_element_type=F32
    )


def normalize(values, gain_row, shift_row):
    centred = values - jnp.mean(values, axis=-1, keepdims=True)
    spread = jnp.mean(centred * centred, axis=-1, keepdims=True)
    factor = lax.rsqrt(spread + EPSILON)
    normed = centred * factor
    return (normed * gain_row + shift_row, normed, factor)


def normalize_back(grad_out, normed, factor, gain_row):
    scaled = grad_out * gain_row
    return factor * (
        scaled
        - jnp.mean(scaled, axis=-1, keepdims=True)
        - normed * jnp.mean(scaled * normed, axis=-1, keepdims=True)
    )


class Wire:
    def __init__(self, send, recv, local=None):
        self.send, self.recv, self.local = send, recv, local
        self.used = self.used_local = 0

    def copy(self, src, dst, device):
        k = self.used
        self.used += 1
        return pltpu.make_async_remote_copy(
            src_ref=src,
            dst_ref=dst,
            send_sem=self.send.at[k],
            recv_sem=self.recv.at[k],
            device_id=device,
            device_id_type=MESH,
        )

    def near(self, src, dst):
        k = self.used_local
        self.used_local += 1
        return pltpu.make_async_copy(src, dst, self.local.at[k])


class Place:
    def __init__(self, sizes):
        self.dp_size, self.ctx_size, self.tp_size = sizes
        self.chips = self.dp_size // 2
        self.dp = lax.axis_index("dp")
        self.ctx = lax.axis_index("ctx")
        self.tp = lax.axis_index("tp")
        self.chip = lax.div(self.dp, 2)
        self.core = lax.rem(self.dp, 2)
        self.sibling = self.chip * 2 + (1 - self.core)

    def ahead(self, i, j):
        return (
            lax.rem(self.chip + i, self.chips) * 2 + self.core,
            lax.rem(self.tp + j, self.tp_size),
        )

    def behind(self, i, j):
        return self.ahead(self.chips - i, self.tp_size - j)

    def offsets(self, over_tp=True):
        return [
            (i, j)
            for i in range(self.chips)
            for j in range(self.tp_size if over_tp else 1)
            if i or j
        ]

    def greet(self, with_ctx):
        barrier = pltpu.get_barrier_semaphore()
        count = 0
        for i, j in self.offsets():
            dp, tp = self.ahead(i, j)
            pl.semaphore_signal(
                barrier, inc=1, device_id={"dp": dp, "tp": tp}, device_id_type=MESH
            )
            count += 1
        pl.semaphore_signal(
            barrier, inc=1, device_id={"dp": self.sibling}, device_id_type=MESH
        )
        count += 1
        if with_ctx:
            for i in range(1, self.ctx_size):
                pl.semaphore_signal(
                    barrier,
                    inc=1,
                    device_id={"ctx": lax.rem(self.ctx + i, self.ctx_size)},
                    device_id_type=MESH,
                )
                count += 1
        pl.semaphore_wait(barrier, count)


def gather_plane_start(place, wire, items):
    flights, done = [], []
    for source, slot, over_tp in items:
        for i, j in place.offsets(over_tp):
            dp, tp = place.ahead(i, j)
            copy = wire.copy(source, slot(place.dp, place.tp), {"dp": dp, "tp": tp})
            copy.start()
            flights.append((copy, slot(*place.behind(i, j))))
    for source, slot, _ in items:
        copy = wire.copy(source, slot(place.dp, place.tp), {"dp": place.sibling})
        copy.start()
        done.append(copy)
        copy = wire.near(source, slot(place.dp, place.tp))
        copy.start()
        done.append(copy)
    return flights, done


def gather_plane_end(place, wire, flights, done):
    for copy, got in flights:
        copy.wait_recv()
        onward = wire.copy(got, got, {"dp": place.sibling})
        onward.start()
        done.append(onward)
    for copy, _ in flights:
        copy.wait_send()
    for copy in done:
        copy.wait()


def plane_copies(place, flags):
    sent = sum(len(place_offsets(place, f)) for f in flags)
    return sent, len(flags)


def place_offsets(sizes, over_tp):
    chips = sizes[0] // 2
    return chips * (sizes[2] if over_tp else 1) - 1


def semaphores(remote, near):
    return [
        pltpu.SemaphoreType.DMA((remote,)),
        pltpu.SemaphoreType.DMA((remote,)),
        pltpu.SemaphoreType.DMA((near,)),
    ]


def comm_params(number):
    return pltpu.CompilerParams(
        collective_id=number, has_side_effects=True, vmem_limit_bytes=48 << 20
    )


def gather_ctx_start(place, wire, source, slot):
    flights = []
    for i in range(1, place.ctx_size):
        copy = wire.copy(
            source,
            slot(place.ctx, place.tp),
            {"ctx": lax.rem(place.ctx + i, place.ctx_size)},
        )
        copy.start()
        flights.append(
            (copy, slot(lax.rem(place.ctx - i + place.ctx_size, place.ctx_size), place.tp))
        )
    return flights


def start_kernel(
    sizes, tokens, weights, mixing, router, cotangent, ints,
    tokens_all, weights_all, mixing_all, router_all, cotangent_all, ints_all, ctx_ints,
    send, recv, local,
):
    place = Place(sizes)
    wire = Wire(send, recv, local)
    place.greet(True)
    rows, lanes = mixing.shape
    half = tokens.shape[1] // place.tp_size
    other_tp = lax.rem(place.tp + 1, 2)

    def token_slot(ctx, tp):
        start = pl.multiple_of(ctx * tokens.shape[1] + tp * half, 16)
        return tokens_all.at[:, pl.ds(start, half), :]

    def at_rows(dp):
        return pl.ds(pl.multiple_of(dp * rows, 16), rows)

    def at_lanes(tp):
        return pl.ds(pl.multiple_of(tp * lanes, 128), lanes)

    mine = tokens.at[:, pl.ds(pl.multiple_of(place.tp * half, 16), half), :]
    token_flights = gather_ctx_start(place, wire, mine, token_slot)
    int_flights = gather_ctx_start(place, wire, ints, lambda ctx, tp: ctx_ints.at[ctx])
    flights, done = gather_plane_start(
        place,
        wire,
        [
            (weights, lambda dp, tp: weights_all.at[:, at_rows(dp), at_lanes(tp)], True),
            (mixing, lambda dp, tp: mixing_all.at[at_rows(dp), at_lanes(tp)], True),
            (ints, lambda dp, tp: ints_all.at[pl.ds(dp * 2, 2)], False),
            (router, lambda dp, tp: router_all.at[dp], False),
            (cotangent, lambda dp, tp: cotangent_all.at[pl.ds(dp * 2, 2)], False),
        ],
    )
    whole = tokens_all.at[:, pl.ds(pl.multiple_of(place.ctx * tokens.shape[1], 16), tokens.shape[1]), :]
    for src, dst in ((tokens, whole), (ints, ctx_ints.at[place.ctx])):
        copy = wire.near(src, dst)
        copy.start()
        done.append(copy)
    for copy, got in token_flights:
        copy.wait_recv()
        onward = wire.copy(got, got, {"tp": other_tp})
        onward.start()
        done.append(onward)
    for copy, _ in int_flights:
        copy.wait()
    for copy, _ in token_flights:
        copy.wait_send()
    gather_plane_end(place, wire, flights, done)


def start_gather(sizes, tokens, weights, mixing, router, cotangent, ints):
    dp, ctx, tp = sizes
    rows, lanes = mixing.shape
    images, block = tokens.shape[:2]
    full, part = place_offsets(sizes, True), place_offsets(sizes, False)
    remote = 3 * (ctx - 1) + 4 * full + 6 * part + 5
    return pl.pallas_call(
        functools.partial(start_kernel, sizes),
        out_shape=(
            jax.ShapeDtypeStruct((images, ctx * block, D), BF16),
            jax.ShapeDtypeStruct((3, dp * rows, tp * lanes), BF16),
            jax.ShapeDtypeStruct((dp * rows, tp * lanes), BF16),
            jax.ShapeDtypeStruct((dp,) + router.shape, BF16),
            jax.ShapeDtypeStruct((dp * images, block, D), BF16),
            jax.ShapeDtypeStruct((dp * images,) + ints.shape[1:], jnp.int32),
            jax.ShapeDtypeStruct((ctx,) + ints.shape, jnp.int32),
        ),
        in_specs=[ANY] * 6,
        out_specs=(ANY,) * 7,
        scratch_shapes=semaphores(remote, 7),
        compiler_params=comm_params(1),
    )(tokens, weights, mixing, router, cotangent, ints)


def expert_in_kernel(sizes, own, gathered, send, recv, local):
    place = Place(sizes)
    wire = Wire(send, recv, local)
    place.greet(False)
    half = own.shape[1]

    def slot(dp, tp):
        return gathered.at[pl.ds(dp * 2, 2), pl.ds(pl.multiple_of(tp * half, 16), half), :]

    flights, done = gather_plane_start(place, wire, [(own, slot, True)])
    gather_plane_end(place, wire, flights, done)


def expert_in_gather(sizes, own):
    dp, ctx, tp = sizes
    images, half = own.shape[:2]
    return pl.pallas_call(
        functools.partial(expert_in_kernel, sizes),
        out_shape=jax.ShapeDtypeStruct((dp * images, tp * half, D), BF16),
        in_specs=[ANY],
        out_specs=ANY,
        scratch_shapes=semaphores(2 * place_offsets(sizes, True) + 1, 1),
        compiler_params=comm_params(2),
    )(own)


def return_kernel(sizes, partial, received, from_sibling, paired, send, recv, local):
    place = Place(sizes)
    wire = Wire(send, recv, local)
    place.greet(False)
    swap = wire.copy(partial.at[1 - place.core], from_sibling, {"dp": place.sibling})
    swap.start()
    swap.wait_recv()
    copies = []
    for i, j in place.offsets() + [(0, 0)]:
        dp, tp = place.ahead(i, j)
        chip = lax.div(dp, 2)
        paired[chip, tp] = (
            partial[place.core, chip, tp].astype(F32) + from_sibling[chip, tp].astype(F32)
        ).astype(BF16)
        index = i * place.tp_size + j
        if index:
            copy = wire.copy(paired.at[chip, tp], received.at[index], {"dp": dp, "tp": tp})
        else:
            copy = wire.near(paired.at[chip, tp], received.at[0])
        copy.start()
        copies.append(copy)
    for copy in copies:
        copy.wait()
    swap.wait_send()


def return_rows(sizes, partial):
    dp, ctx, tp = sizes
    count, lanes = partial.shape[3:]
    chips = dp // 2
    return pl.pallas_call(
        functools.partial(return_kernel, sizes),
        out_shape=jax.ShapeDtypeStruct((chips * tp, count, lanes), BF16),
        in_specs=[IN_VMEM],
        out_specs=ANY,
        scratch_shapes=[
            pltpu.VMEM((chips, tp, count, lanes), BF16),
            pltpu.VMEM((chips, tp, count, lanes), BF16),
        ]
        + semaphores(chips * tp, 1),
        compiler_params=comm_params(3),
    )(partial)


def heads_kernel(sizes, own, stats, gathered, stats_all, send, recv, local):
    place = Place(sizes)
    wire = Wire(send, recv, local)
    place.greet(True)
    half = own.shape[1]
    other_tp = lax.rem(place.tp + 1, 2)

    def rows_slot(ctx, tp):
        start = pl.multiple_of((ctx * place.tp_size + tp) * half, 16)
        return gathered.at[:, pl.ds(start, half), :]

    def stats_slot(ctx, tp):
        return stats_all.at[ctx * place.tp_size + tp]

    done, flights = [], []
    for source, slot in ((own, rows_slot), (stats, stats_slot)):
        flights += gather_ctx_start(place, wire, source, slot)
    for source, slot in ((own, rows_slot), (stats, stats_slot)):
        spot = slot(place.ctx, place.tp)
        for copy in (wire.copy(source, spot, {"tp": other_tp}), wire.near(source, spot)):
            copy.start()
            done.append(copy)
    for copy, got in flights:
        copy.wait_recv()
        onward = wire.copy(got, got, {"tp": other_tp})
        onward.start()
        done.append(onward)
    for copy, _ in flights:
        copy.wait_send()
    for copy in done:
        copy.wait()


def heads_gather(sizes, own, stats):
    dp, ctx, tp = sizes
    images, half, lanes = own.shape
    return pl.pallas_call(
        functools.partial(heads_kernel, sizes),
        out_shape=(
            jax.ShapeDtypeStruct((images, ctx * tp * half, lanes), BF16),
            jax.ShapeDtypeStruct((ctx * tp,) + stats.shape, BF16),
        ),
        in_specs=[ANY] * 2,
        out_specs=(ANY,) * 2,
        scratch_shapes=semaphores(2 * (2 * (ctx - 1) + 1), 2),
        compiler_params=comm_params(4),
    )(own, stats)


def add_rounded(*parts):
    total = parts[0].astype(F32)
    for part in parts[1:]:
        total = total + part.astype(F32)
    return total.astype(BF16)


def finish_kernel(
    sizes, first, second, small, out_own, grad_own,
    first_all, second_all, small_all, out_all, grad_all,
    second_got, small_got, second_sum, small_sum,
    first_end, second_end, small_end,
    first_mid, second_mid, small_mid,
    first_stage, second_stage, small_stage,
    first_final, second_final, small_final,
    send, recv, local,
):
    place = Place(sizes)
    wire = Wire(send, recv, local)
    plane = place.dp_size * place.tp_size
    me = place.dp * place.tp_size + place.tp
    is_mid = jnp.logical_and(place.ctx >= 1, place.ctx <= 2)
    is_end = jnp.logical_not(is_mid)
    inner = lax.div(place.ctx, 2)
    outer_half = 1 - inner
    partner = jnp.where(is_mid, inner * 3, 1 + inner)
    other_mid = 2 - inner
    other_tp = lax.rem(place.tp + 1, 2)
    half = out_own.shape[1]
    experts = first.shape[0]

    barrier = pltpu.get_barrier_semaphore()
    peers = []
    for k in range(1, plane):
        peer = lax.rem(me + k, plane)
        peers.append((lax.div(peer, place.tp_size), lax.rem(peer, place.tp_size)))
        pl.semaphore_signal(
            barrier, inc=1, device_id={"dp": peers[-1][0], "tp": peers[-1][1]}, device_id_type=MESH
        )
    pl.semaphore_signal(barrier, inc=1, device_id={"ctx": partner}, device_id_type=MESH)

    @pl.when(is_mid)
    def _():
        pl.semaphore_signal(barrier, inc=1, device_id={"ctx": other_mid}, device_id_type=MESH)

    pl.semaphore_wait(barrier, plane + jnp.where(is_mid, 1, 0))

    swap = wire.copy(second.at[other_tp], second_got, {"tp": other_tp})
    swap.start()
    spread = []
    for k, (dp, tp) in enumerate(peers):
        copy = wire.copy(
            small.at[dp * place.tp_size + tp], small_got.at[k], {"dp": dp, "tp": tp}
        )
        copy.start()
        spread.append(copy)
    outs = []
    for own, gathered in ((out_own, out_all), (grad_own, grad_all)):
        spot = gathered.at[:, pl.ds(pl.multiple_of(place.tp * half, 16), half), :]
        outs.append(wire.copy(own, spot, {"tp": other_tp}))
        outs.append(wire.near(own, spot))

    chunks = [
        (
            first.at[e], first_end.at[e], first_mid.at[e], first_stage.at[e],
            first_final.at[e], functools.partial(lambda e, dp, tp: first_all.at[dp, tp, e], e),
        )
        for e in range(experts)
    ]
    chunks.append(
        (second_sum, second_end, second_mid, second_stage, second_final,
         lambda dp, tp: second_all.at[dp, tp])
    )
    chunks.append(
        (small_sum, small_end, small_mid, small_stage, small_final,
         lambda dp, tp: small_all.at[dp, tp])
    )

    flows = []
    for mine, end, mid, stage, final, slot in chunks:
        flows.append(
            dict(
                outer=wire.copy(mine.at[outer_half], end.at[outer_half], {"ctx": partner}),
                inner=wire.copy(mine.at[inner], end.at[inner], {"ctx": partner}),
                cross=wire.copy(stage, mid, {"ctx": other_mid}),
                back=wire.copy(final.at[inner], final.at[inner], {"ctx": partner}),
                share=wire.copy(final.at[inner], final.at[inner], {"ctx": other_mid}),
                pass_on=wire.copy(final.at[outer_half], final.at[outer_half], {"ctx": partner}),
            )
        )

    def send_ends(k):
        @pl.when(is_end)
        def _():
            flows[k]["outer"].start()
            flows[k]["inner"].start()

    for k in range(experts):
        send_ends(k)
    swap.wait()
    second_sum[...] = add_rounded(second[place.tp], second_got[...])
    send_ends(experts)
    for copy in spread:
        copy.wait()
    total = small[me].astype(F32)
    for k in range(plane - 1):
        total = total + small_got[k].astype(F32)
    small_sum[...] = total.astype(BF16).reshape(small_sum.shape)
    send_ends(experts + 1)

    def mid_first(k):
        mine, end, mid, stage, final, slot = chunks[k]

        @pl.when(is_mid)
        def _():
            flows[k]["outer"].wait_recv()
            stage[...] = add_rounded(mine[outer_half], end[outer_half])
            flows[k]["cross"].start()

    def mid_second(k):
        mine, end, mid, stage, final, slot = chunks[k]

        @pl.when(is_mid)
        def _():
            flows[k]["inner"].wait_recv()
            flows[k]["cross"].wait_recv()
            final[inner] = add_rounded(mine[inner], end[inner], mid[...])
            flows[k]["share"].start()
            flows[k]["back"].start()

    def settle(k):
        @pl.when(is_mid)
        def _():
            flows[k]["share"].wait_recv()
            flows[k]["pass_on"].start()

        @pl.when(is_end)
        def _():
            flows[k]["back"].wait_recv()
            flows[k]["pass_on"].wait_recv()

    squared = place.chips == 2 and place.tp_size == 2
    done = []
    plane_flights = []

    def plane_send(k):
        final, slot = chunks[k][4], chunks[k][5]
        spot = slot(place.dp, place.tp)
        flights = []
        for i, j in place.offsets():
            if squared and i and j:
                continue
            dp, tp = place.ahead(i, j)
            copy = wire.copy(final, spot, {"dp": dp, "tp": tp})
            copy.start()
            flights.append((copy, i, j))
        for copy in (wire.copy(final, spot, {"dp": place.sibling}), wire.near(final, spot)):
            copy.start()
            done.append(copy)
        plane_flights.append(flights)

    def to_sibling(ref):
        copy = wire.copy(ref, ref, {"dp": place.sibling})
        copy.start()
        done.append(copy)

    diagonals = []

    def plane_forward(k):
        slot = chunks[k][5]
        for copy, i, j in plane_flights[k]:
            copy.wait_recv()
            got = slot(*place.behind(i, j))
            if squared:
                part = 0 if j else 1
                dp, tp = place.ahead(1 - i, 1 - j)
                onward = wire.copy(got.at[part], got.at[part], {"dp": dp, "tp": tp})
                onward.start()
                diagonals.append((onward, slot(*place.behind(1, 1)).at[part]))
            to_sibling(got)
            copy.wait_send()

    def plane_diagonal():
        while diagonals:
            copy, got = diagonals.pop(0)
            copy.wait_recv()
            to_sibling(got)
            copy.wait_send()

    count = len(chunks)
    for k in range(count + 3):
        if k < count:
            mid_first(k)
        if 1 <= k < count + 1:
            mid_second(k - 1)
        if 2 <= k < count + 2:
            settle(k - 2)
            plane_send(k - 2)
        if k == 2:
            for copy in outs:
                copy.start()
        if k >= 3:
            plane_diagonal()
            plane_forward(k - 3)
    plane_diagonal()

    @pl.when(is_end)
    def _():
        for flow in flows:
            flow["outer"].wait_send()
            flow["inner"].wait_send()

    @pl.when(is_mid)
    def _():
        for flow in flows:
            for name in ("cross", "back", "share", "pass_on"):
                flow[name].wait_send()

    for copy in outs + done:
        copy.wait()


def finish(sizes, first, second, small, out_own, grad_own):
    dp, ctx, tp = sizes
    experts, _, width, lanes = first.shape
    part = second.shape[1:]
    rows = small.shape[1]
    small_part = (2, rows // 2, 128)
    plane = dp * tp
    images, half = out_own.shape[:2]
    chunks = experts + 2
    offsets = place_offsets(sizes, True)
    per_chunk = 6 + 2 * offsets + 1 + 4
    remote = chunks * per_chunk + plane + 2

    def buffers(make):
        return [make((experts, 2, width, lanes), 1), make(part, 0), make(small_part, 0)]

    def full(shape, lead):
        return pltpu.VMEM(shape, BF16)

    def one(shape, lead):
        return pltpu.VMEM(shape[:lead] + shape[lead + 1 :], BF16)

    return pl.pallas_call(
        functools.partial(finish_kernel, sizes),
        out_shape=(
            jax.ShapeDtypeStruct((dp, tp) + first.shape, BF16),
            jax.ShapeDtypeStruct((dp, tp) + part, BF16),
            jax.ShapeDtypeStruct((dp, tp) + small_part, BF16),
            jax.ShapeDtypeStruct((images, tp * half, D), BF16),
            jax.ShapeDtypeStruct((images, tp * half, D), BF16),
        ),
        in_specs=[IN_VMEM] * 3 + [ANY] * 2,
        out_specs=(ANY,) * 5,
        scratch_shapes=[
            pltpu.VMEM(part, BF16),
            pltpu.VMEM((plane - 1, rows, 128), BF16),
            pltpu.VMEM(part, BF16),
            pltpu.VMEM(small_part, BF16),
        ]
        + buffers(full)
        + buffers(one)
        + buffers(one)
        + buffers(full)
        + semaphores(remote, chunks + 2),
        compiler_params=comm_params(5),
    )(first, second, small, out_own, grad_own)


def put_lanes(columns, width):
    lane = lax.broadcasted_iota(jnp.int32, (columns[0].shape[0], width), 1)
    total = jnp.zeros((columns[0].shape[0], width), F32)
    for k, column in enumerate(columns):
        total = jnp.where(lane == k, column, total)
    return total


def half_masks():
    lane = lax.broadcasted_iota(jnp.int32, (1, 2 * HD), 1)
    even = (lane < HD).astype(F32)
    return even, 1.0 - even


def stack_pair(rows, masks, factor=1.0):
    wide = rows.astype(F32) * factor
    return jnp.concatenate([wide * masks[0], wide * masks[1]], axis=0).astype(BF16)


def join_pair(rows, masks):
    half = rows.shape[0] // 2
    return rows[:half] * masks[0] + rows[half:] * masks[1]


def attend_kernel(
    place, tokens, weights, mixing, live_keys, picks, attend_low, attend_high, mixing_low,
    mixing_high, gains,
    joined, own_in, own_lift, head_mix_out, log_out, mixing_lift_out, hidden_out, expert_in_out,
    lift_scratch,
):
    images, seq = tokens.shape[:2]
    half = head_mix_out.shape[0] // images
    own_start = pl.multiple_of(place[0], 16)
    block = seq // 2

    def project(k, _):
        i, r = lax.div(k, 2), pl.multiple_of(lax.rem(k, 2) * block, 16)
        rows = tokens[i, pl.ds(r, block), :].astype(F32)
        normed = normalize(rows, gains[0:1, :], gains[1:2, :])[0].astype(BF16)
        lift = (times_transposed(normed, attend_low[...]) * picks[pl.ds(i, 1), :]).astype(BF16)
        lift_scratch[i, pl.ds(r, block), :] = lift
        for p in range(3):
            joined[p, i, pl.ds(r, block), :] = (
                matmul(normed, weights[p]) + matmul(lift, attend_high[p])
            ).astype(BF16)
        return 0

    lax.fori_loop(0, images * 2, project, 0)
    masks = half_masks()
    scale = HD**-0.5
    mix_parts = []
    for i in range(images):
        open_keys = live_keys[i : i + 1, :] > 0
        rows = tokens[i, pl.ds(own_start, half), :].astype(F32)
        own_in[i] = normalize(rows, gains[0:1, :], gains[1:2, :])[0].astype(BF16)
        own_lift[i] = lift_scratch[i, pl.ds(own_start, half), :]
        logs = []
        for j in range(HEADS // 2):
            lanes = slice(j * 2 * HD, (j + 1) * 2 * HD)
            q = stack_pair(joined[0, i, pl.ds(own_start, half), lanes], masks, scale)
            scores = times_transposed(q, joined[1, i, :, lanes])
            scores = jnp.where(open_keys, scores, MASKED)
            top = jnp.max(scores, axis=-1, keepdims=True)
            powers = jnp.exp(scores - top)
            total = jnp.sum(powers, axis=-1, keepdims=True)
            weights_att = (powers * (1.0 / total)).astype(BF16)
            mixed = join_pair(matmul(weights_att, joined[2, i, :, lanes]), masks)
            head_mix_out[i * half : (i + 1) * half, lanes] = mixed.astype(BF16)
            log = jnp.maximum(top + jnp.log(total), -1e29)
            logs += [log[:half], log[half:]]
        log_out[i * half : (i + 1) * half, :] = put_lanes(logs, 128)
        mix = head_mix_out[i * half : (i + 1) * half, :]
        lift = (times_transposed(mix, mixing_low[...]) * picks[i : i + 1, :]).astype(BF16)
        mixing_lift_out[i * half : (i + 1) * half, :] = lift
        hidden = rows + times_transposed(mix, mixing[...]) + matmul(lift, mixing_high[...])
        hidden_out[i * half : (i + 1) * half, :] = hidden
        expert_in_out[i] = normalize(hidden, gains[2:3, :], gains[3:4, :])[0].astype(BF16)


def attend(half, place, *operands):
    images, seq = operands[0].shape[:2]
    count = images * half

    def out(*shape, dtype=BF16):
        return jax.ShapeDtypeStruct(shape, dtype)

    return pl.pallas_call(
        attend_kernel,
        out_shape=(
            out(3, images, seq, D),
            out(images, half, D),
            out(images, half, WIDTH),
            out(count, D),
            out(count, 128, dtype=F32),
            out(count, WIDTH),
            out(count, D, dtype=F32),
            out(images, half, D),
        ),
        in_specs=[pl.BlockSpec(memory_space=pltpu.SMEM)] + [IN_VMEM] * len(operands),
        out_specs=(IN_VMEM,) * 8,
        scratch_shapes=[pltpu.VMEM((images, seq, WIDTH), BF16)],
        compiler_params=pltpu.CompilerParams(vmem_limit_bytes=48 << 20),
    )(place, *operands)


def experts_kernel(
    place, rows_all, cot_all, ints, picks, picks_t, router_t, router_low, router_high_t,
    up_weight, down_weight, first_a, first_b, second_a, second_b,
    first_grads, second_grads, partial,
    table, rows_in, grad_slots, gates, payload,
):
    e = pl.program_id(0)
    last = pl.num_programs(0) - 1
    experts, count = rows_in.shape[:2]
    images, block = rows_all.shape[:2]
    owned = place[1]
    slots = experts * SLOTS
    half = block // second_grads.shape[0]

    @pl.when(e == 0)
    def _():
        def dispatch(i, _):
            rows = rows_all[i]
            lift = times_transposed(router_low[...], rows) * picks_t[i]
            logits = times_transposed(router_t[...], rows) + matmul(
                router_high_t[...], lift.astype(BF16)
            )
            powers = jnp.exp(logits - jnp.max(logits, axis=0, keepdims=True))
            probs = powers / jnp.sum(powers, axis=0, keepdims=True)
            numbers = ints[i]
            expert = lax.broadcasted_iota(jnp.int32, (EXPERTS, block), 0)
            slot = lax.broadcasted_iota(jnp.int32, (slots, block), 0)
            hot = jnp.zeros((slots, block), F32)
            gated = jnp.zeros((slots, block), F32)
            for k in range(TOP):
                route, place_in = numbers[k : k + 1, :], numbers[TOP + k : TOP + k + 1, :]
                gate = jnp.sum(jnp.where(expert == route, probs, 0.0), axis=0, keepdims=True)
                local = route - owned
                here = (local >= 0) & (local < experts) & (place_in < CAP)
                target = jnp.where(here, local * SLOTS + place_in, -1)
                match = slot == target
                hot = jnp.where(match, 1.0, hot)
                gated = jnp.where(match, gate, gated)
            hot = hot.astype(BF16)
            table[i] = hot
            gate_column = jnp.broadcast_to(jnp.sum(gated, axis=1, keepdims=True), (slots, 128))
            picked = matmul(hot, rows).astype(BF16)
            grads = matmul(hot, cot_all[i]).astype(BF16)
            at = pl.ds(pl.multiple_of(i * SLOTS, SLOTS), SLOTS)
            for n in range(experts):
                part = slice(n * SLOTS, (n + 1) * SLOTS)
                rows_in[n, at, :] = picked[part]
                grad_slots[n, at, :] = grads[part]
                gates[n, at, :] = gate_column[part]
            return 0

        lax.fori_loop(0, images, dispatch, 0)

    rows = rows_in[e]
    grads = grad_slots[e].astype(F32)
    gate = gates[e][:, 0:1]
    sets = jnp.broadcast_to(picks[...][:, None, :], (images, SLOTS, WIDTH)).reshape(count, WIDTH)
    a_first, b_first = first_a[:, 0].reshape(WIDTH, D), first_b[:, 0].reshape(WIDTH, -1)
    a_second, b_second = second_a[:, 0].reshape(WIDTH, -1), second_b[:, 0].reshape(WIDTH, D)
    lifted = (times_transposed(rows, a_first) * sets).astype(BF16)
    before = matmul(rows, up_weight[0]) + matmul(lifted, b_first)
    phi = 0.5 * (1.0 + lax.erf(before * SQRT_HALF))
    active = (before * phi).astype(BF16)
    slope = phi + before * (INV_ROOT_TWO_PI * jnp.exp(-0.5 * before * before))
    lowered = (times_transposed(active, a_second) * sets).astype(BF16)
    out = matmul(active, down_weight[0]) + matmul(lowered, b_second)
    grad_out = (grads * gate).astype(BF16)
    grad_lowered = (times_transposed(grad_out, b_second) * sets).astype(BF16)
    grad_active = times_transposed(grad_out, down_weight[0]) + matmul(grad_lowered, a_second)
    grad_before = (grad_active * slope).astype(BF16)
    grad_lifted = (times_transposed(grad_before, b_first) * sets).astype(BF16)
    grad_rows = times_transposed(grad_before, up_weight[0]) + matmul(grad_lifted, a_first)
    first_grads[0, 0] = inner_rows(lifted, grad_before).astype(BF16)
    first_grads[0, 1] = inner_rows(grad_lowered, active).astype(BF16)
    pieces = second_grads.shape[0]
    lanes = D // pieces
    for number, value in (
        (0, inner_rows(grad_lifted, rows)),
        (1, inner_rows(lowered, grad_out)),
    ):
        for t in range(pieces):
            second_grads[t, number, e] = value[:, t * lanes : (t + 1) * lanes].astype(BF16)
    lane = lax.broadcasted_iota(jnp.int32, (count, 128), 1)
    gate_grads = jnp.sum(out * grads, axis=1, keepdims=True)
    gated_out = (out * gate).astype(BF16).reshape(images, SLOTS, D)
    grad_rows = grad_rows.astype(BF16).reshape(images, SLOTS, D)
    gate_grads = jnp.where(lane == owned + e, gate_grads, 0.0).astype(BF16)
    gate_grads = gate_grads.reshape(images, SLOTS, 128)
    at = pl.ds(pl.multiple_of(e * SLOTS, SLOTS), SLOTS)
    payload[:, at, 0:D] = gated_out
    payload[:, at, D : 2 * D] = grad_rows
    payload[:, at, 2 * D :] = gate_grads

    @pl.when(e == last)
    def _():
        def combine(i, _):
            dp, local = lax.div(i, 2), lax.rem(i, 2)
            rows = inner_rows(table[i], payload[i]).astype(BF16)
            core, chip = lax.rem(dp, 2), lax.div(dp, 2)
            for t in range(partial.shape[2]):
                partial[core, chip, t, local] = rows[t * half : (t + 1) * half]
            return 0

        lax.fori_loop(0, images, combine, 0)


def run_experts(
    sizes, place, rows_all, cot_all, ints, picks, picks_t, router_t, router_low, router_high_t,
    up_weight, down_weight, first_a, first_b, second_a, second_b,
):
    dp, ctx, tp = sizes
    experts, _, hidden = up_weight.shape
    images, block = rows_all.shape[:2]
    half = block // tp
    lanes = 2 * D + 128
    count = images * SLOTS

    def whole(array):
        return pl.BlockSpec(array.shape, lambda e, place: (0,) * array.ndim)

    def adapter(size, split):
        return pl.BlockSpec(
            (SETS, 1, RANK, size),
            lambda e, place: (0, place[1] + e, 0, place[2] if split else 0),
        )

    second_shape = (tp, 2, experts, WIDTH, D // tp)
    partial_shape = (2, dp // 2, tp, images // dp, half, lanes)
    return pl.pallas_call(
        experts_kernel,
        grid_spec=pltpu.PrefetchScalarGridSpec(
            num_scalar_prefetch=1,
            grid=(experts,),
            in_specs=[
                whole(a)
                for a in (
                    rows_all, cot_all, ints, picks, picks_t, router_t, router_low, router_high_t,
                )
            ]
            + [
                pl.BlockSpec((1, D, hidden), lambda e, place: (e, 0, 0)),
                pl.BlockSpec((1, hidden, D), lambda e, place: (e, 0, 0)),
                adapter(D, False),
                adapter(hidden, True),
                adapter(hidden, True),
                adapter(D, False),
            ],
            out_specs=[
                pl.BlockSpec((1, 2, WIDTH, hidden), lambda e, place: (e, 0, 0, 0)),
                pl.BlockSpec(second_shape, lambda e, place: (0,) * 5),
                pl.BlockSpec(partial_shape, lambda e, place: (0,) * 6),
            ],
            scratch_shapes=[
                pltpu.VMEM((images, experts * SLOTS, block), BF16),
                pltpu.VMEM((experts, count, D), BF16),
                pltpu.VMEM((experts, count, D), BF16),
                pltpu.VMEM((experts, count, 128), F32),
                pltpu.VMEM((images, experts * SLOTS, lanes), BF16),
            ],
        ),
        out_shape=[
            jax.ShapeDtypeStruct((experts, 2, WIDTH, hidden), BF16),
            jax.ShapeDtypeStruct(second_shape, BF16),
            jax.ShapeDtypeStruct(partial_shape, BF16),
        ],
        compiler_params=pltpu.CompilerParams(vmem_limit_bytes=56 << 20),
    )(
        place, rows_all, cot_all, ints, picks, picks_t, router_t, router_low, router_high_t,
        up_weight, down_weight, first_a, first_b, second_a, second_b,
    )


def split_sum(values, ones):
    high = values.astype(BF16)
    low = (values - high.astype(F32)).astype(BF16)
    return matmul(high, ones) + matmul(low, ones)


def middle_kernel(
    place, received, hidden_in, expert_in, cotangent, live, picks, router_t, router_low,
    router_high, mixing, mixing_low, mixing_high, head_mix, mixing_lift, logs, gains,
    layer_out, grad_hidden_out, heads_out, stats_out, delta_out, tiles,
):
    images, half = expert_in.shape[:2]
    count = images * half
    start = pl.multiple_of(place[3], 16)
    total = received[0].astype(F32)
    for k in range(1, received.shape[0]):
        total = total + received[k].astype(F32)
    hidden = hidden_in[...]
    layer_out[...] = (hidden + total[:, :D]).astype(BF16).reshape(images, half, D)
    grad_probs = total[:, 2 * D : 2 * D + EXPERTS]
    own_sets = jnp.concatenate(
        [jnp.broadcast_to(picks[i : i + 1, :], (half, WIDTH)) for i in range(images)], axis=0
    )
    grad_output = jnp.concatenate(
        [cotangent[i, pl.ds(start, half), :] for i in range(images)], axis=0
    ).astype(F32) * live[...]
    rows = expert_in[...].reshape(count, D)
    router_lift = (times_transposed(rows, router_low[...]) * own_sets).astype(BF16)
    logits = times_transposed(rows, router_t[...]) + matmul(router_lift, router_high[...])
    powers = jnp.exp(logits - jnp.max(logits, axis=-1, keepdims=True))
    gate_probs = powers / jnp.sum(powers, axis=-1, keepdims=True)
    grad_logits = (
        gate_probs * (grad_probs - jnp.sum(grad_probs * gate_probs, axis=-1, keepdims=True))
    ).astype(BF16)
    grad_router_lift = (times_transposed(grad_logits, router_high[...]) * own_sets).astype(BF16)
    grad_expert_in = (
        total[:, D : 2 * D]
        + matmul(grad_logits, router_t[...])
        + matmul(grad_router_lift, router_low[...])
    )
    _, unit, factor = normalize(hidden, gains[2:3, :], gains[3:4, :])
    grad_hidden = grad_output + normalize_back(grad_expert_in, unit, factor, gains[2:3, :])
    grad_hidden_out[...] = grad_hidden
    grad_attended = grad_hidden.astype(BF16)
    grad_mixing_lift = (times_transposed(grad_attended, mixing_high[...]) * own_sets).astype(BF16)
    grad_heads = (
        matmul(grad_attended, mixing[...]) + matmul(grad_mixing_lift, mixing_low[...])
    ).astype(BF16)
    heads_out[...] = grad_heads.reshape(images, half, D)
    mix = head_mix[...]
    lane = lax.broadcasted_iota(jnp.int32, (D, 128), 1)
    head = lax.div(lax.broadcasted_iota(jnp.int32, (D, 128), 0), HD)
    ones = (lane == head).astype(F32).astype(BF16)
    delta = split_sum(grad_heads.astype(F32) * mix.astype(F32), ones)
    delta_out[...] = delta
    log = logs[...]
    for i in range(images):
        part = slice(i * half, (i + 1) * half)
        pad = jnp.zeros((128 - half, 128), F32)
        stats = [jnp.concatenate([v[part], pad], axis=0).T[:HEADS] for v in (log, delta)]
        row = 0
        for rest, number in zip(stats, (3, 2)):
            for _ in range(number):
                high = rest.astype(BF16)
                stats_out[i, row : row + HEADS, :] = high
                rest = rest - high.astype(F32)
                row += HEADS
    products = (
        inner_rows(grad_mixing_lift, mix),
        inner_rows(mixing_lift[...], grad_attended),
        inner_rows(grad_router_lift, rows),
    )
    tile = 0
    for product in products:
        for k in range(D // 128):
            tiles[tile * WIDTH : (tile + 1) * WIDTH, :] = product[
                :, k * 128 : (k + 1) * 128
            ].astype(BF16)
            tile += 1
    wide_logits = jnp.concatenate(
        [grad_logits, jnp.zeros((count, 128 - EXPERTS), BF16)], axis=1
    )
    tiles[tile * WIDTH : (tile + 1) * WIDTH, :] = inner_rows(router_lift, wide_logits).astype(BF16)


def middle(place, *operands):
    images, half = operands[2].shape[:2]
    count = images * half
    tiles = 3 * (D // 128) + 1
    return pl.pallas_call(
        middle_kernel,
        out_shape=(
            jax.ShapeDtypeStruct((images, half, D), BF16),
            jax.ShapeDtypeStruct((count, D), F32),
            jax.ShapeDtypeStruct((images, half, D), BF16),
            jax.ShapeDtypeStruct((images, 5 * HEADS, 128), BF16),
            jax.ShapeDtypeStruct((count, 128), F32),
            jax.ShapeDtypeStruct((tiles * WIDTH, 128), BF16),
        ),
        in_specs=[pl.BlockSpec(memory_space=pltpu.SMEM)] + [IN_VMEM] * len(operands),
        out_specs=(IN_VMEM,) * 6,
        compiler_params=pltpu.CompilerParams(vmem_limit_bytes=48 << 20),
    )(place, *operands)


def attend_back_kernel(
    place, joined, heads_all, stats_all, heads, logs, delta, live_keys, live_own, tokens, own_in,
    own_lift, grad_hidden, weights, attend_low, attend_high, picks, gains, tiles_in,
    tokens_grad, small, grads,
):
    images, seq = joined.shape[1:3]
    half = heads.shape[1]
    own_start = pl.multiple_of(place[0], 16)
    start = pl.multiple_of(place[3], 16)
    own = pl.ds(own_start, half)
    masks = half_masks()
    scale = HD**-0.5
    blocks = seq // half
    for i in range(images):
        part = slice(i * half, (i + 1) * half)
        open_keys = live_keys[i : i + 1, :] > 0
        open_own = live_own[part] > 0
        open_own = jnp.concatenate([open_own, open_own], axis=0)
        stats = jnp.concatenate(
            [stats_all[n, i][:, :half].astype(F32) for n in range(blocks)], axis=1
        )
        log_t = stats[0:HEADS] + stats[HEADS : 2 * HEADS] + stats[2 * HEADS : 3 * HEADS]
        delta_t = stats[3 * HEADS : 4 * HEADS] + stats[4 * HEADS :]
        log_own, delta_own = logs[part], delta[part]
        for j in range(HEADS // 2):
            lanes = slice(j * 2 * HD, (j + 1) * 2 * HD)
            q_all, k_all, v_all = (joined[p, i, :, lanes] for p in range(3))
            g_all = heads_all[i, :, lanes]

            def column(values):
                return jnp.concatenate(
                    [values[:, 2 * j : 2 * j + 1], values[:, 2 * j + 1 : 2 * j + 2]], axis=0
                )

            def row(values):
                return jnp.concatenate(
                    [
                        jnp.broadcast_to(values[2 * j + n : 2 * j + n + 1, :], (half, seq))
                        for n in range(2)
                    ],
                    axis=0,
                )

            q = stack_pair(joined[0, i, own, lanes], masks, scale)
            g = stack_pair(heads[i, :, lanes], masks)
            scores = jnp.where(open_keys, times_transposed(q, k_all), MASKED)
            probs = jnp.exp(scores - column(log_own))
            grad_probs = times_transposed(g, v_all)
            grad_scores = (probs * (grad_probs - column(delta_own))).astype(BF16)
            grads[0, part, lanes] = (
                join_pair(matmul(grad_scores, k_all), masks) * scale
            ).astype(BF16)
            k = stack_pair(joined[1, i, own, lanes], masks, scale)
            v = stack_pair(joined[2, i, own, lanes], masks)
            scores = jnp.where(open_own, times_transposed(k, q_all), MASKED)
            probs = jnp.exp(scores - row(log_t))
            grad_probs = times_transposed(v, g_all)
            grad_scores = (probs * (grad_probs - row(delta_t))).astype(BF16)
            grads[1, part, lanes] = (
                join_pair(matmul(grad_scores, q_all), masks) * scale
            ).astype(BF16)
            grads[2, part, lanes] = join_pair(matmul(probs.astype(BF16), g_all), masks).astype(
                BF16
            )
    own_sets = jnp.concatenate(
        [jnp.broadcast_to(picks[i : i + 1, :], (half, WIDTH)) for i in range(images)], axis=0
    )
    lift = times_transposed(grads[0], attend_high[0])
    into = times_transposed(grads[0], weights[0])
    for p in range(1, 3):
        lift = lift + times_transposed(grads[p], attend_high[p])
        into = into + times_transposed(grads[p], weights[p])
    lift = (lift * own_sets).astype(BF16)
    into = into + matmul(lift, attend_low[...])
    flat = jnp.concatenate(
        [tokens[i, pl.ds(start, half), :] for i in range(images)], axis=0
    ).astype(F32)
    _, unit, factor = normalize(flat, gains[0:1, :], gains[1:2, :])
    result = grad_hidden[...] + normalize_back(into, unit, factor, gains[0:1, :])
    tokens_grad[...] = result.astype(BF16).reshape(images, half, D)
    rows_in = own_in[...].reshape(images * half, D)
    lift_in = own_lift[...].reshape(images * half, WIDTH)
    products = [inner_rows(lift_in, grads[p]) for p in range(3)] + [inner_rows(lift, rows_in)]
    tile = 0
    for product in products:
        for n in range(D // 128):
            small[tile * WIDTH : (tile + 1) * WIDTH, :] = product[
                :, n * 128 : (n + 1) * 128
            ].astype(BF16)
            tile += 1
    done = tile * WIDTH + tiles_in.shape[0]
    small[tile * WIDTH : done, :] = tiles_in[...]
    if done < small.shape[0]:
        small[done:, :] = jnp.zeros((small.shape[0] - done, 128), BF16)


def attend_back(small_rows, place, *operands):
    images, half = operands[3].shape[:2]
    count = images * half
    return pl.pallas_call(
        attend_back_kernel,
        out_shape=(
            jax.ShapeDtypeStruct((images, half, D), BF16),
            jax.ShapeDtypeStruct((small_rows, 128), BF16),
        ),
        in_specs=[pl.BlockSpec(memory_space=pltpu.SMEM)] + [IN_VMEM] * len(operands),
        out_specs=(IN_VMEM,) * 2,
        scratch_shapes=[pltpu.VMEM((3, count, D), BF16)],
        compiler_params=pltpu.CompilerParams(vmem_limit_bytes=48 << 20),
    )(place, *operands)


def assemble_kernel(
    first, second, small, up, down_t, narrow_t, narrow,
    attend_down, attend_up, mixing_down, mixing_up, router_down, router_up,
):
    lanes, part = first.shape[-1], second.shape[-1]
    for tp in range(first.shape[1]):
        for half, out in ((0, up), (1, down_t)):
            out[:, 0, :, tp * lanes : (tp + 1) * lanes] = (
                first[0, tp, 0, half].astype(F32).reshape(SETS, RANK, lanes)
            )
        for half, out in ((0, narrow_t), (1, narrow)):
            out[:, 0, :, tp * part : (tp + 1) * part] = (
                second[0, tp, half, 0].astype(F32).reshape(SETS, RANK, part)
            )

    @pl.when(pl.program_id(0) == 0)
    def _():
        def tile(k):
            return small[k * WIDTH : (k + 1) * WIDTH, :].astype(F32).reshape(SETS, RANK, 128)

        count = D // 128
        for p in range(3):
            for k in range(count):
                attend_up[:, p, :, k * 128 : (k + 1) * 128] = tile(p * count + k)
        for p, out in enumerate((attend_down, mixing_down, mixing_up, router_down)):
            for k in range(count):
                out[:, :, k * 128 : (k + 1) * 128] = tile((p + 3) * count + k)
        router_up[...] = tile(7 * count)[:, :, :EXPERTS]


def assemble(first, second, small):
    dp, tp, experts, _, width, lanes = first.shape
    part = second.shape[-1]

    def split(e):
        return lax.div(e, experts), lax.rem(e, experts)

    def expert_out(size):
        return (
            jax.ShapeDtypeStruct((SETS, EXPERTS, RANK, size), F32),
            pl.BlockSpec((SETS, 1, RANK, size), lambda e: (0, e, 0, 0)),
        )

    def whole_out(*shape):
        return (
            jax.ShapeDtypeStruct(shape, F32),
            pl.BlockSpec(shape, lambda e: (0,) * len(shape)),
        )

    outs = (
        [expert_out(FF)] * 2
        + [expert_out(D)] * 2
        + [whole_out(SETS, RANK, D), whole_out(SETS, 3, RANK, D)]
        + [whole_out(SETS, RANK, D)] * 3
        + [whole_out(SETS, RANK, EXPERTS)]
    )
    return pl.pallas_call(
        assemble_kernel,
        grid=(EXPERTS,),
        out_shape=[out[0] for out in outs],
        in_specs=[
            pl.BlockSpec(
                (1, tp, 1, 2, width, lanes), lambda e: (split(e)[0], 0, split(e)[1], 0, 0, 0)
            ),
            pl.BlockSpec(
                (1, tp, 2, 1, width, part), lambda e: (split(e)[0], 0, 0, split(e)[1], 0, 0)
            ),
            pl.BlockSpec(small.shape, lambda e: (0, 0)),
        ],
        out_specs=[out[1] for out in outs],
        compiler_params=pltpu.CompilerParams(vmem_limit_bytes=32 << 20),
    )(first, second, small)


def per_device(
    sizes,
    tokens,
    cotangent,
    routes,
    slot_index,
    token_mask,
    image_mask,
    adapter_set,
    first_gain,
    first_shift,
    second_gain,
    second_shift,
    attend_weight,
    mixing_weight,
    router_weight,
    expand_weight,
    shrink_weight,
    attend_down,
    attend_up,
    mixing_down,
    mixing_up,
    router_down,
    router_up,
    expand_down,
    expand_up,
    shrink_down,
    shrink_up,
):
    dp_size, ctx_size, tp_size = sizes
    plane = dp_size * tp_size
    images, block = tokens.shape[:2]
    half = block // tp_size
    count = images * half
    seq = ctx_size * block
    all_images = dp_size * images
    local_experts, _, hidden_half = expand_weight.shape
    ctx_index, tp_index, dp_index = (lax.axis_index(a) for a in ("ctx", "tp", "dp"))
    place = jnp.stack(
        [
            ctx_index * block + tp_index * half,
            dp_index * local_experts,
            tp_index,
            tp_index * half,
        ]
    ).astype(jnp.int32)

    live = token_mask * image_mask[:, None]
    ints = jnp.concatenate(
        [
            jnp.transpose(routes, (0, 2, 1)),
            jnp.transpose(slot_index, (0, 2, 1)),
            live[:, None, :],
            jnp.broadcast_to(adapter_set[:, None, None], (images, 3, block)),
        ],
        axis=1,
    )
    tokens_all, weights_all, mixing_all, router_parts, cotangent_all, ints_all, ctx_ints = (
        start_gather(
            sizes,
            tokens,
            jnp.transpose(attend_weight, (1, 0, 2)),
            mixing_weight,
            jnp.transpose(router_weight, (1, 0)),
            cotangent,
            ints,
        )
    )
    router_t = jnp.transpose(router_parts, (1, 0, 2)).reshape(EXPERTS, D)

    attend_low = jnp.transpose(attend_down, (0, 2, 1)).reshape(WIDTH, D)
    attend_high = jnp.transpose(attend_up, (2, 0, 1, 3)).reshape(3, WIDTH, D)
    mixing_low = jnp.transpose(mixing_down, (0, 2, 1)).reshape(WIDTH, D)
    mixing_high = mixing_up.reshape(WIDTH, D)
    router_low = jnp.transpose(router_down, (0, 2, 1)).reshape(WIDTH, D)
    router_high = router_up.reshape(WIDTH, EXPERTS)
    gains = jnp.stack([first_gain, first_shift, second_gain, second_shift])

    def picker(sets):
        return (sets[:, None] == jnp.arange(WIDTH)[None, :] // RANK).astype(F32)

    own_picks = picker(adapter_set)
    key_live = jnp.transpose(ctx_ints[:, :, 4, :], (1, 0, 2)).reshape(images, seq)
    own_live = (
        lax.dynamic_slice_in_dim(live, tp_index * half, half, 1).reshape(count, 1).astype(F32)
    )
    joined, own_in, own_lift, head_mix, logs, mixing_lift, hidden, expert_in = attend(
        half, place, tokens_all, weights_all, mixing_all, key_live, own_picks, attend_low,
        attend_high, mixing_low, mixing_high, gains,
    )
    expert_in_all = expert_in_gather(sizes, expert_in)
    picks = picker(ints_all[:, 5, 0])
    first_grads, second_grads, partial = run_experts(
        sizes, place, expert_in_all, cotangent_all, ints_all, picks, picks[:, :, None], router_t,
        router_low, jnp.transpose(router_high), expand_weight, shrink_weight,
        jnp.transpose(expand_down, (0, 1, 3, 2)),
        expand_up,
        jnp.transpose(shrink_down, (0, 1, 3, 2)),
        shrink_up,
    )
    received = return_rows(
        sizes, partial.reshape(2, dp_size // 2, tp_size, count, partial.shape[-1])
    )
    layer_out, grad_hidden, heads, stats, delta, tiles = middle(
        place, received, hidden, expert_in, cotangent, own_live, own_picks, router_t, router_low,
        router_high, mixing_all, mixing_low, mixing_high, head_mix, mixing_lift, logs, gains,
    )
    heads_all, stats_all = heads_gather(sizes, heads, stats)
    needed = (7 * (D // 128) + 1) * WIDTH
    rows = -(-needed // (plane * 16)) * 16
    tokens_grad, small = attend_back(
        plane * rows, place, joined, heads_all, stats_all, heads, logs, delta, key_live, own_live,
        tokens, own_in, own_lift, grad_hidden, weights_all, attend_low, attend_high, own_picks,
        gains, tiles,
    )
    first_all, second_all, small_all, out_all, grad_all = finish(
        sizes, first_grads, second_grads, small.reshape(plane, rows, 128), layer_out, tokens_grad
    )
    wide = assemble(first_all, second_all, small_all.reshape(plane * rows, 128))

    def flipped(values):
        return jnp.swapaxes(values, -1, -2)

    return (
        out_all,
        grad_all,
        flipped(wide[4]),
        jnp.transpose(wide[5], (0, 2, 1, 3)),
        flipped(wide[6]),
        wide[7],
        flipped(wide[8]),
        wide[9],
        flipped(wide[2]),
        wide[0],
        flipped(wide[1]),
        wide[3],
    )


def solution(mesh):
    sizes = (mesh.shape["dp"], mesh.shape["ctx"], mesh.shape["tp"])
    tokens_spec = P("dp", "ctx", None)
    in_specs = (
        (tokens_spec,) * 4
        + (P("dp", "ctx"), P("dp"), P("dp"))
        + (P(),) * 4
        + (P("dp", None, "tp"), P("dp", "tp"), P("dp", None))
        + (P("dp", None, "tp"), P("dp", "tp", None))
        + (P(),) * 10
    )
    out_specs = (tokens_spec,) * 2 + (P(),) * 10
    return jax.shard_map(
        functools.partial(per_device, sizes),
        mesh=mesh,
        in_specs=in_specs,
        out_specs=out_specs,
        check_vma=False,
    )
```

profile of v0, /device:TPU:1, one launch (start us, length us, event | category | flops | bytes accessed | tf_op | source)
XLA Modules:
  0.0 263.7 jit_solution(16665541780472590600)
XLA Ops:
  0.7 0.1 pad_add_fusion.1.place
  0.7 0.7 compare_convert_fusion.2.picks
  1.5 0.8 broadcast_multiply_fusion
  2.2 0.1 dynamic-slice_convert_fusion
  2.3 1.4 copy.52.router_high_t
  3.7 0.7 pad_maximum_fusion.gains
  4.4 0.7 broadcast_in_dim.5
  5.1 0.7 pad_add_fusion.ints
  5.9 0.1 convert_element_type.18.live.live_own
  6.0 0.9 copy.49
  7.0 0.0 copy-start.4
  7.0 1.0 copy-done.4
  7.9 1.0 copy-done.8
  8.9 0.9 copy-done.19
  9.8 0.8 copy-done.22
  10.7 0.7 copy-done.26
  11.4 27.9 %shard_map.337 = (bf16[2,640,512]{2,1,0:T(8,128)(2,1)S(1)}, bf16[3,512,512]{2,1,0:T(8,128)(2,1)S(1)}, bf16[512,512]{1,0:T(8,128)(2,1)S(1)}, bf16[4,16,128]{2,1,0...) custom-call(bf16[2,160,512]{2,1,0:T(8,128)(2,1)S(1)} %copy-done.4, ...), custom_call_target="tpu_custom_call" | custom-call | tf_op jit(solution)/shard_map/pallas_call | solution.py:270
  39.3 0.0 copy-start.3
  39.3 1.0 copy-done.3
  40.4 1.1 copy-done.6
  41.4 0.2 slice_reduce_fusion
  41.7 0.7 compare_convert_fusion.1.picks
  42.4 0.1 reshape.161.live_keys
  42.5 0.6 copy_bitcast_fusion.router_t
  43.1 0.8 compare_convert_fusion.picks_t
  43.9 1.3 copy-done.7
  45.2 0.8 copy-done.12
  46.0 0.8 copy-done.14
  46.9 0.8 copy-done.16
  47.7 12.2 %shard_map.338 = (bf16[3,2,640,512]{3,2,1,0:T(8,128)(2,1)}, bf16[2,80,512]{2,1,0:T(8,128)(2,1)S(1)}, bf16[2,80,64]{2,1,0:T(8,128)(2,1)S(1)}, bf16[160,512]{1,0:T...) custom-call(s32[4]{0:T(128)S(1)} %pad_add_fusion.1.place, ...), custom_call_target="tpu_custom_call" | custom-call | tf_op jit(solution)/shard_map/pallas_call | solution.py:763
  59.9 12.5 %shard_map.339.rows_all = bf16[8,160,512]{2,1,0:T(8,128)(2,1)S(1)} custom-call(bf16[2,80,512]{2,1,0:T(8,128)(2,1)S(1)} %get-tuple-element.59.own.expert_in), custom_call_target="tpu_custom_call" | custom-call | tf_op jit(solution)/shard_map/pallas_call | solution.py:304
  72.4 0.0 copy-done.24
  72.4 0.0 copy-done.21
  72.4 0.0 copy-start.1
  72.4 1.0 copy-done.1
  73.5 0.0 copy-start.20
  73.5 0.0 copy-start.23
  73.5 25.2 %shard_map.340 = (bf16[4,2,64,1024]{3,2,1,0:T(8,128)(2,1)}, bf16[2,2,4,64,256]{4,3,2,1,0:T(8,128)(2,1)}, bf16[2,2,2,2,80,1152]{5,4,3,2,1,0:T(8,128)(2,1)}) custom-call(s32[4]{0:T(128)} %copy-done.24, bf16[8,160,512]{2,1,0:T(8,128)(2,1)} %copy-done.1, bf16[8,160,512]{2,1,0:T(8,128)(2,1)} %copy-done.3, s32[8,8,160]{2,1,0:T(8,128)} %copy-done.21, ...), custom_call_target="tpu_custom_call" | custom-call | tf_op jit(solution)/shard_map/pallas_call | solution.py:910
  98.7 0.0 copy-start.25
  98.7 0.0 copy-start.2
  98.7 1.8 copy-done.2
  100.6 22.6 %shard_map.341.received = bf16[4,160,1152]{2,1,0:T(8,128)(2,1)S(1)} custom-call(bf16[2,2,2,160,1152]{4,3,2,1,0:T(8,128)(2,1)S(1)} %bitcast.49), custom_call_target="tpu_custom_call" | custom-call | tf_op jit(solution)/shard_map/pallas_call | solution.py:344
  123.1 0.0 copy-done.9
  123.1 0.0 copy-done.15
  123.1 0.0 copy-done.17
  123.2 0.0 copy-done.18
  123.2 0.0 copy-done.20
  123.2 0.0 copy-done.23
  123.2 0.0 copy-done.25
  123.2 2.4 shard_map.342
  125.6 22.5 %shard_map.343 = (bf16[2,640,512]{2,1,0:T(8,128)(2,1)S(1)}, bf16[8,2,40,128]{3,2,1,0:T(8,128)(2,1)S(1)}) custom-call(bf16[2,80,512]{2,1,0:T(8,128)(2,1)S(1)} %get-tuple-element.71.own.heads, bf16[2,40,128]{2,1,0:T(8,128)(2,1)S(1)} %get-tuple-element.72.stats), custom_call_target="tpu_custom_call" | custom-call | tf_op jit(solution)/shard_map/pallas_call | solution.py:394
  148.1 0.0 copy-done.5
  148.1 0.0 copy-done.13
  148.1 0.0 copy-start.10
  148.2 0.0 copy-start.11
  148.2 8.0 %shard_map.344 = (bf16[2,80,512]{2,1,0:T(8,128)(2,1)S(1)}, bf16[1920,128]{1,0:T(8,128)(2,1)S(1)}) custom-call(s32[4]{0:T(128)S(1)} %copy-done.25, bf16[3,2,640,512]{3,2,1,0:T(8,128)(2,1)} %get-tuple-element.65.joined, bf16[2,640,512]{2,1,0:T(8,128)(2,1)S(1)} %get-tuple-element.73.heads_all, bf16[8,2,40,128]{3,2,1,0:T(8,128)(2,1)S(1)} %get-tuple-element.74.stats_all, ...), custom_call_target="tpu_custom_call" | custom-call | tf_op jit(solution)/shard_map/pallas_call | solution.py:1158
  156.2 0.0 copy-done.10
  156.2 0.0 copy-done.11
  156.2 92.6 %shard_map.345 = (bf16[4,2,4,2,64,1024]{5,4,3,2,1,0:T(8,128)(2,1)}, bf16[4,2,2,4,64,256]{5,4,3,2,1,0:T(8,128)(2,1)S(1)}, bf16[4,2,2,120,128]{4,3,2,1,0:T(8,128)(...) custom-call(bf16[4,2,64,1024]{3,2,1,0:T(8,128)(2,1)S(1)} %copy-done.10, ...), custom_call_target="tpu_custom_call" | custom-call | tf_op jit(solution)/shard_map/pallas_call | solution.py:651
  248.8 0.0 copy-start
  248.8 3.4 %copy-done = bf16[4,2,4,2,64,1024]{5,4,3,2,1,0:T(8,128)(2,1)S(1)} copy-done((bf16[4,2,4,2,64,1024]{5,4,3,2,1,0:T(8,128)(2,1)S(1)}, bf16[4,2,4,2,64,1024]{5,4,3,2,1,0:T(8,128)(2,1)}, u32[]{:S(2)}) %copy-start) | copy-done | bytes 8388632
  252.2 10.1 %shard_map.346 = (f32[4,16,16,2048]{3,2,1,0:T(8,128)}, f32[4,16,16,2048]{3,2,1,0:T(8,128)}, f32[4,16,16,512]{3,2,1,0:T(8,128)}, f32[4,16,16,512]{3,2,1,0:T(8,128...) custom-call(bf16[4,2,4,2,64,1024]{5,4,3,2,1,0:T(8,128)(2,1)S(1)} %co, ...), custom_call_target="tpu_custom_call" | custom-call | tf_op jit(solution)/shard_map/pallas_call | solution.py:1227
  262.2 0.7 copy.62
  263.0 0.7 copy.63
  (22 shorter events, 0.1 us)
Async XLA Ops:
  0.7 71.7 %copy-start.24 = (s32[4]{0:T(128)}, s32[4]{0:T(128)S(1)}, u32[]{:S(2)}) copy-start(s32[4]{0:T(128)S(1)} %pad_add_fusion.1.place) | copy-start | bytes 52
  7.0 1.0 copy-start.4
  7.9 1.0 copy-start.8
  8.9 0.9 copy-start.19
  9.8 0.8 copy-start.22
  10.7 0.7 copy-start.26
  39.3 1.1 copy-start.3
  40.4 1.1 copy-start.6
  41.4 31.0 %copy-start.21 = (s32[8,8,160]{2,1,0:T(8,128)}, s32[8,8,160]{2,1,0:T(8,128)S(1)}, u32[]{:S(2)}) copy-start(s32[8,8,160]{2,1,0:T(8,128)S(1)} %get-tuple-element.61.ints) | copy-start | bytes 122884
  43.9 1.3 copy-start.7
  45.2 0.8 copy-start.12
  46.0 0.8 copy-start.14
  46.9 0.8 copy-start.16
  72.4 1.1 copy-start.1
  73.5 49.7 %copy-start.9 = (bf16[2,160,512]{2,1,0:T(8,128)(2,1)S(1)}, bf16[2,160,512]{2,1,0:T(8,128)(2,1)}, u32[]{:S(2)}) copy-start(bf16[2,160,512]{2,1,0:T(8,128)(2,1)} %cotangent.3) | copy-start | bytes 983044
  73.5 49.7 %copy-start.15 = (bf16[4,512,16]{1,2,0:T(8,128)(2,1)S(1)}, bf16[4,512,16]{1,2,0:T(8,128)(2,1)}, u32[]{:S(2)}) copy-start(bf16[4,512,16]{1,2,0:T(8,128)(2,1)} %param.44) | copy-start | bytes 196612
  73.5 49.7 %copy-start.17 = (bf16[4,16,512]{2,1,0:T(8,128)(2,1)S(1)}, bf16[4,16,512]{2,1,0:T(8,128)(2,1)}, u32[]{:S(2)}) copy-start(bf16[4,16,512]{2,1,0:T(8,128)(2,1)} %param.45) | copy-start | bytes 196612
  73.5 49.7 %copy-start.18 = (bf16[4,512,16]{1,2,0:T(8,128)(2,1)S(1)}, bf16[4,512,16]{1,2,0:T(8,128)(2,1)}, u32[]{:S(2)}) copy-start(bf16[4,512,16]{1,2,0:T(8,128)(2,1)} %param.46) | copy-start | bytes 196612
  73.5 49.7 %copy-start.20 = (bf16[16,512]{1,0:T(8,128)(2,1)S(1)}, bf16[16,512]{1,0:T(8,128)(2,1)}, u32[]{:S(2)}) copy-start(bf16[16,512]{1,0:T(8,128)(2,1)} %copy_bitcast_fusion.router_t) | copy-start | bytes 49156
  73.5 49.7 %copy-start.23 = (bf16[4,16,16]{2,1,0:T(8,128)(2,1)S(1)}, bf16[4,16,16]{2,1,0:T(8,128)(2,1)}, u32[]{:S(2)}) copy-start(bf16[4,16,16]{2,1,0:T(8,128)(2,1)} %param.47) | copy-start | bytes 6148
  98.7 24.5 %copy-start.25 = (s32[4]{0:T(128)S(1)}, s32[4]{0:T(128)}, u32[]{:S(2)}) copy-start(s32[4]{0:T(128)} %copy-done.24) | copy-start | bytes 52
  98.7 1.8 copy-start.2
  100.5 47.6 %copy-start.5 = (bf16[2,160,512]{2,1,0:T(8,128)(2,1)S(1)}, bf16[2,160,512]{2,1,0:T(8,128)(2,1)}, u32[]{:S(2)}) copy-start(bf16[2,160,512]{2,1,0:T(8,128)(2,1)} %tokens.3) | copy-start | bytes 983044
  100.5 47.6 %copy-start.13 = (bf16[4,512,16]{1,2,0:T(8,128)(2,1)S(1)}, bf16[4,512,16]{1,2,0:T(8,128)(2,1)}, u32[]{:S(2)}) copy-start(bf16[4,512,16]{1,2,0:T(8,128)(2,1)} %param.42) | copy-start | bytes 196612
  148.1 8.0 %copy-start.10 = (bf16[4,2,64,1024]{3,2,1,0:T(8,128)(2,1)S(1)}, bf16[4,2,64,1024]{3,2,1,0:T(8,128)(2,1)}, u32[]{:S(2)}) copy-start(bf16[4,2,64,1024]{3,2,1,0:T(8,128)(2,1)} %get-tuple-element.63.first) | copy-start | bytes 3145732
  148.2 8.0 %copy-start.11 = (bf16[2,2,4,64,256]{4,3,2,1,0:T(8,128)(2,1)S(1)}, bf16[2,2,4,64,256]{4,3,2,1,0:T(8,128)(2,1)}, u32[]{:S(2)}) copy-start(bf16[2,2,4,64,256]{4,3,2,1,0:T(8,128)(2,1)} %get-tuple-element.64.second) | copy-start | bytes 1572868
  248.8 3.4 %copy-start = (bf16[4,2,4,2,64,1024]{5,4,3,2,1,0:T(8,128)(2,1)S(1)}, bf16[4,2,4,2,64,1024]{5,4,3,2,1,0:T(8,128)(2,1)}, u32[]{:S(2)}) copy-start(bf16[4,2,4,2,64,1024]{5,4,3,2,1,0:T(8,128)(2,1)} %get-tuple-element.85.first) | copy-start | bytes 25165828
where the time goes:
time: 265 us; the launch traced here: 264 us
  Pallas kernels  236 us (89%)
  local copies, waits for them, and re-layouts  22.2 us (8%)
  other arithmetic  4.57 us (2%)
    pallas_call x1, Pallas kernels, finish(): pl.pallas_call(functools.partial(finish_kernel, sizes), out_shape=(jax.Sh...  92.6 us
    pallas_call x1, Pallas kernels, start_gather(): pl.pallas_call(functools.partial(start_kernel, sizes), out_shape=(jax.Sha...  27.9 us
    pallas_call x1, Pallas kernels, run_experts(): pl.pallas_call(experts_kernel, grid_spec=pltpu.PrefetchScalarGridSpec(num...  25.2 us
    pallas_call x1, Pallas kernels, return_rows(): pl.pallas_call(functools.partial(return_kernel, sizes), out_shape=jax.Sha...  22.6 us
    pallas_call x1, Pallas kernels, heads_gather(): pl.pallas_call(functools.partial(heads_kernel, sizes), out_shape=(jax.Sha...  22.5 us
    unnamed x57, local copies, waits for them, and re-layouts  18.1 us
    pallas_call x1, Pallas kernels, expert_in_gather(): pl.pallas_call(functools.partial(expert_in_kernel, sizes), out_shape=jax....  12.5 us
    pallas_call x1, Pallas kernels, attend(): pl.pallas_call(attend_kernel, out_shape=(out(3, images, seq, D), out(imag...  12.2 us

commit v1 on v0

--- a/solution.py
+++ b/solution.py
@@ -311,367 +311,11 @@
     )(own)
 
 
-def return_kernel(sizes, partial, received, from_sibling, paired, send, recv, local):
-    place = Place(sizes)
-    wire = Wire(send, recv, local)
-    place.greet(False)
-    swap = wire.copy(partial.at[1 - place.core], from_sibling, {"dp": place.sibling})
-    swap.start()
-    swap.wait_recv()
-    copies = []
-    for i, j in place.offsets() + [(0, 0)]:
-        dp, tp = place.ahead(i, j)
-        chip = lax.div(dp, 2)
-        paired[chip, tp] = (
-            partial[place.core, chip, tp].astype(F32) + from_sibling[chip, tp].astype(F32)
-        ).astype(BF16)
-        index = i * place.tp_size + j
-        if index:
-            copy = wire.copy(paired.at[chip, tp], received.at[index], {"dp": dp, "tp": tp})
-        else:
-            copy = wire.near(paired.at[chip, tp], received.at[0])
-        copy.start()
-        copies.append(copy)
-    for copy in copies:
-        copy.wait()
-    swap.wait_send()
-
-
-def return_rows(sizes, partial):
-    dp, ctx, tp = sizes
-    count, lanes = partial.shape[3:]
-    chips = dp // 2
-    return pl.pallas_call(
-        functools.partial(return_kernel, sizes),
-        out_shape=jax.ShapeDtypeStruct((chips * tp, count, lanes), BF16),
-        in_specs=[IN_VMEM],
-        out_specs=ANY,
-        scratch_shapes=[
-            pltpu.VMEM((chips, tp, count, lanes), BF16),
-            pltpu.VMEM((chips, tp, count, lanes), BF16),
-        ]
-        + semaphores(chips * tp, 1),
-        compiler_params=comm_params(3),
-    )(partial)
-
-
-def heads_kernel(sizes, own, stats, gathered, stats_all, send, recv, local):
-    place = Place(sizes)
-    wire = Wire(send, recv, local)
-    place.greet(True)
-    half = own.shape[1]
-    other_tp = lax.rem(place.tp + 1, 2)
-
-    def rows_slot(ctx, tp):
-        start = pl.multiple_of((ctx * place.tp_size + tp) * half, 16)
-        return gathered.at[:, pl.ds(start, half), :]
-
-    def stats_slot(ctx, tp):
-        return stats_all.at[ctx * place.tp_size + tp]
-
-    done, flights = [], []
-    for source, slot in ((own, rows_slot), (stats, stats_slot)):
-        flights += gather_ctx_start(place, wire, source, slot)
-    for source, slot in ((own, rows_slot), (stats, stats_slot)):
-        spot = slot(place.ctx, place.tp)
-        for copy in (wire.copy(source, spot, {"tp": other_tp}), wire.near(source, spot)):
-            copy.start()
-            done.append(copy)
-    for copy, got in flights:
-        copy.wait_recv()
-        onward = wire.copy(got, got, {"tp": other_tp})
-        onward.start()
-        done.append(onward)
-    for copy, _ in flights:
-        copy.wait_send()
-    for copy in done:
-        copy.wait()
-
-
-def heads_gather(sizes, own, stats):
-    dp, ctx, tp = sizes
-    images, half, lanes = own.shape
-    return pl.pallas_call(
-        functools.partial(heads_kernel, sizes),
-        out_shape=(
-            jax.ShapeDtypeStruct((images, ctx * tp * half, lanes), BF16),
-            jax.ShapeDtypeStruct((ctx * tp,) + stats.shape, BF16),
-        ),
-        in_specs=[ANY] * 2,
-        out_specs=(ANY,) * 2,
-        scratch_shapes=semaphores(2 * (2 * (ctx - 1) + 1), 2),
-        compiler_params=comm_params(4),
-    )(own, stats)
-
-
 def add_rounded(*parts):
     total = parts[0].astype(F32)
     for part in parts[1:]:
         total = total + part.astype(F32)
     return total.astype(BF16)
-
-
-def finish_kernel(
-    sizes, first, second, small, out_own, grad_own,
-    first_all, second_all, small_all, out_all, grad_all,
-    second_got, small_got, second_sum, small_sum,
-    first_end, second_end, small_end,
-    first_mid, second_mid, small_mid,
-    first_stage, second_stage, small_stage,
-    first_final, second_final, small_final,
-    send, recv, local,
-):
-    place = Place(sizes)
-    wire = Wire(send, recv, local)
-    plane = place.dp_size * place.tp_size
-    me = place.dp * place.tp_size + place.tp
-    is_mid = jnp.logical_and(place.ctx >= 1, place.ctx <= 2)
-    is_end = jnp.logical_not(is_mid)
-    inner = lax.div(place.ctx, 2)
-    outer_half = 1 - inner
-    partner = jnp.where(is_mid, inner * 3, 1 + inner)
-    other_mid = 2 - inner
-    other_tp = lax.rem(place.tp + 1, 2)
-    half = out_own.shape[1]
-    experts = first.shape[0]
-
-    barrier = pltpu.get_barrier_semaphore()
-    peers = []
-    for k in range(1, plane):
-        peer = lax.rem(me + k, plane)
-        peers.append((lax.div(peer, place.tp_size), lax.rem(peer, place.tp_size)))
-        pl.semaphore_signal(
-            barrier, inc=1, device_id={"dp": peers[-1][0], "tp": peers[-1][1]}, device_id_type=MESH
-        )
-    pl.semaphore_signal(barrier, inc=1, device_id={"ctx": partner}, device_id_type=MESH)
-
-    @pl.when(is_mid)
-    def _():
-        pl.semaphore_signal(barrier, inc=1, device_id={"ctx": other_mid}, device_id_type=MESH)
-
-    pl.semaphore_wait(barrier, plane + jnp.where(is_mid, 1, 0))
-
-    swap = wire.copy(second.at[other_tp], second_got, {"tp": other_tp})
-    swap.start()
-    spread = []
-    for k, (dp, tp) in enumerate(peers):
-        copy = wire.copy(
-            small.at[dp * place.tp_size + tp], small_got.at[k], {"dp": dp, "tp": tp}
-        )
-        copy.start()
-        spread.append(copy)
-    outs = []
-    for own, gathered in ((out_own, out_all), (grad_own, grad_all)):
-        spot = gathered.at[:, pl.ds(pl.multiple_of(place.tp * half, 16), half), :]
-        outs.append(wire.copy(own, spot, {"tp": other_tp}))
-        outs.append(wire.near(own, spot))
-
-    chunks = [
-        (
-            first.at[e], first_end.at[e], first_mid.at[e], first_stage.at[e],
-            first_final.at[e], functools.partial(lambda e, dp, tp: first_all.at[dp, tp, e], e),
-        )
-        for e in range(experts)
-    ]
-    chunks.append(
-        (second_sum, second_end, second_mid, second_stage, second_final,
-         lambda dp, tp: second_all.at[dp, tp])
-    )
-    chunks.append(
-        (small_sum, small_end, small_mid, small_stage, small_final,
-         lambda dp, tp: small_all.at[dp, tp])
-    )
-
-    flows = []
-    for mine, end, mid, stage, final, slot in chunks:
-        flows.append(
-            dict(
-                outer=wire.copy(mine.at[outer_half], end.at[outer_half], {"ctx": partner}),
-                inner=wire.copy(mine.at[inner], end.at[inner], {"ctx": partner}),
-                cross=wire.copy(stage, mid, {"ctx": other_mid}),
-                back=wire.copy(final.at[inner], final.at[inner], {"ctx": partner}),
-                share=wire.copy(final.at[inner], final.at[inner], {"ctx": other_mid}),
-                pass_on=wire.copy(final.at[outer_half], final.at[outer_half], {"ctx": partner}),
-            )
-        )
-
-    def send_ends(k):
-        @pl.when(is_end)
-        def _():
-            flows[k]["outer"].start()
-            flows[k]["inner"].start()
-
-    for k in range(experts):
-        send_ends(k)
-    swap.wait()
-    second_sum[...] = add_rounded(second[place.tp], second_got[...])
-    send_ends(experts)
-    for copy in spread:
-        copy.wait()
-    total = small[me].astype(F32)
-    for k in range(plane - 1):
-        total = total + small_got[k].astype(F32)
-    small_sum[...] = total.astype(BF16).reshape(small_sum.shape)
-    send_ends(experts + 1)
-
-    def mid_first(k):
-        mine, end, mid, stage, final, slot = chunks[k]
-
-        @pl.when(is_mid)
-        def _():
-            flows[k]["outer"].wait_recv()
-            stage[...] = add_rounded(mine[outer_half], end[outer_half])
-            flows[k]["cross"].start()
-
-    def mid_second(k):
-        mine, end, mid, stage, final, slot = chunks[k]
-
-        @pl.when(is_mid)
-        def _():
-            flows[k]["inner"].wait_recv()
-            flows[k]["cross"].wait_recv()
-            final[inner] = add_rounded(mine[inner], end[inner], mid[...])
-            flows[k]["share"].start()
-            flows[k]["back"].start()
-
-    def settle(k):
-        @pl.when(is_mid)
-        def _():
-            flows[k]["share"].wait_recv()
-            flows[k]["pass_on"].start()
-
-        @pl.when(is_end)
-        def _():
-            flows[k]["back"].wait_recv()
-            flows[k]["pass_on"].wait_recv()
-
-    squared = place.chips == 2 and place.tp_size == 2
-    done = []
-    plane_flights = []
-
-    def plane_send(k):
-        final, slot = chunks[k][4], chunks[k][5]
-        spot = slot(place.dp, place.tp)
-        flights = []
-        for i, j in place.offsets():
-            if squared and i and j:
-                continue
-            dp, tp = place.ahead(i, j)
-            copy = wire.copy(final, spot, {"dp": dp, "tp": tp})
-            copy.start()
-            flights.append((copy, i, j))
-        for copy in (wire.copy(final, spot, {"dp": place.sibling}), wire.near(final, spot)):
-            copy.start()
-            done.append(copy)
-        plane_flights.append(flights)
-
-    def to_sibling(ref):
-        copy = wire.copy(ref, ref, {"dp": place.sibling})
-        copy.start()
-        done.append(copy)
-
-    diagonals = []
-
-    def plane_forward(k):
-        slot = chunks[k][5]
-        for copy, i, j in plane_flights[k]:
-            copy.wait_recv()
-            got = slot(*place.behind(i, j))
-            if squared:
-                part = 0 if j else 1
-                dp, tp = place.ahead(1 - i, 1 - j)
-                onward = wire.copy(got.at[part], got.at[part], {"dp": dp, "tp": tp})
-                onward.start()
-                diagonals.append((onward, slot(*place.behind(1, 1)).at[part]))
-            to_sibling(got)
-            copy.wait_send()
-
-    def plane_diagonal():
-        while diagonals:
-            copy, got = diagonals.pop(0)
-            copy.wait_recv()
-            to_sibling(got)
-            copy.wait_send()
-
-    count = len(chunks)
-    for k in range(count + 3):
-        if k < count:
-            mid_first(k)
-        if 1 <= k < count + 1:
-            mid_second(k - 1)
-        if 2 <= k < count + 2:
-            settle(k - 2)
-            plane_send(k - 2)
-        if k == 2:
-            for copy in outs:
-                copy.start()
-        if k >= 3:
-            plane_diagonal()
-            plane_forward(k - 3)
-    plane_diagonal()
-
-    @pl.when(is_end)
-    def _():
-        for flow in flows:
-            flow["outer"].wait_send()
-            flow["inner"].wait_send()
-
-    @pl.when(is_mid)
-    def _():
-        for flow in flows:
-            for name in ("cross", "back", "share", "pass_on"):
-                flow[name].wait_send()
-
-    for copy in outs + done:
-        copy.wait()
-
-
-def finish(sizes, first, second, small, out_own, grad_own):
-    dp, ctx, tp = sizes
-    experts, _, width, lanes = first.shape
-    part = second.shape[1:]
-    rows = small.shape[1]
-    small_part = (2, rows // 2, 128)
-    plane = dp * tp
-    images, half = out_own.shape[:2]
-    chunks = experts + 2
-    offsets = place_offsets(sizes, True)
-    per_chunk = 6 + 2 * offsets + 1 + 4
-    remote = chunks * per_chunk + plane + 2
-
-    def buffers(make):
-        return [make((experts, 2, width, lanes), 1), make(part, 0), make(small_part, 0)]
-
-    def full(shape, lead):
-        return pltpu.VMEM(shape, BF16)
-
-    def one(shape, lead):
-        return pltpu.VMEM(shape[:lead] + shape[lead + 1 :], BF16)
-
-    return pl.pallas_call(
-        functools.partial(finish_kernel, sizes),
-        out_shape=(
-            jax.ShapeDtypeStruct((dp, tp) + first.shape, BF16),
-            jax.ShapeDtypeStruct((dp, tp) + part, BF16),
-            jax.ShapeDtypeStruct((dp, tp) + small_part, BF16),
-            jax.ShapeDtypeStruct((images, tp * half, D), BF16),
-            jax.ShapeDtypeStruct((images, tp * half, D), BF16),
-        ),
-        in_specs=[IN_VMEM] * 3 + [ANY] * 2,
-        out_specs=(ANY,) * 5,
-        scratch_shapes=[
-            pltpu.VMEM(part, BF16),
-            pltpu.VMEM((plane - 1, rows, 128), BF16),
-            pltpu.VMEM(part, BF16),
-            pltpu.VMEM(small_part, BF16),
-        ]
-        + buffers(full)
-        + buffers(one)
-        + buffers(one)
-        + buffers(full)
-        + semaphores(remote, chunks + 2),
-        compiler_params=comm_params(5),
-    )(first, second, small, out_own, grad_own)
 
 
 def put_lanes(columns, width):
@@ -868,9 +512,9 @@
     gate_grads = jnp.where(lane == owned + e, gate_grads, 0.0).astype(BF16)
     gate_grads = gate_grads.reshape(images, SLOTS, 128)
     at = pl.ds(pl.multiple_of(e * SLOTS, SLOTS), SLOTS)
-    payload[:, at, 0:D] = gated_out
-    payload[:, at, D : 2 * D] = grad_rows
-    payload[:, at, 2 * D :] = gate_grads
+    payload[:, at, 0:D] = grad_rows
+    payload[:, at, D : D + 128] = gate_grads
+    payload[:, at, D + 128 :] = gated_out
 
     @pl.when(e == last)
     def _():
@@ -957,25 +601,324 @@
     return matmul(high, ones) + matmul(low, ones)
 
 
-def middle_kernel(
-    place, received, hidden_in, expert_in, cotangent, live, picks, router_t, router_low,
-    router_high, mixing, mixing_low, mixing_high, head_mix, mixing_lift, logs, gains,
-    layer_out, grad_hidden_out, heads_out, stats_out, delta_out, tiles,
+class Chain:
+    def __init__(self, place, wire, sources, slots):
+        self.place, n = place, place.ctx_size
+        self.steps = n - 1
+        other_tp = lax.rem(place.tp + 1, 2)
+        self.right, self.left, self.over_right, self.over_left = {}, {}, {}, {}
+        self.own = []
+        for source, slot in zip(sources, slots):
+            here = slot(place.ctx, place.tp)
+            self.own.append(wire.copy(source, here, {"tp": other_tp}))
+            self.own.append(wire.near(source, here))
+        for s in range(1, n):
+            back = [slot(jnp.maximum(place.ctx - (s - 1), 0), place.tp) for slot in slots]
+            ahead = [slot(jnp.minimum(place.ctx + (s - 1), n - 1), place.tp) for slot in slots]
+            got_right = [slot(jnp.maximum(place.ctx - s, 0), place.tp) for slot in slots]
+            got_left = [slot(jnp.minimum(place.ctx + s, n - 1), place.tp) for slot in slots]
+            to_right = {"ctx": jnp.minimum(place.ctx + 1, n - 1)}
+            to_left = {"ctx": jnp.maximum(place.ctx - 1, 0)}
+            self.right[s] = [
+                wire.copy(a if s == 1 else b, b, to_right) for a, b in zip(sources, back)
+            ]
+            self.left[s] = [
+                wire.copy(a if s == 1 else b, b, to_left) for a, b in zip(sources, ahead)
+            ]
+            self.over_right[s] = [wire.copy(b, b, {"tp": other_tp}) for b in got_right]
+            self.over_left[s] = [wire.copy(b, b, {"tp": other_tp}) for b in got_left]
+
+    def sends_right(self, s):
+        return jnp.logical_and(self.place.ctx >= s - 1, self.place.ctx < self.steps)
+
+    def sends_left(self, s):
+        return jnp.logical_and(self.place.ctx <= self.steps + 1 - s, self.place.ctx > 0)
+
+    def gets_right(self, s):
+        return self.place.ctx >= s
+
+    def gets_left(self, s):
+        return self.place.ctx <= self.steps - s
+
+    @staticmethod
+    def all_of(copies, verb):
+        for copy in copies:
+            getattr(copy, verb)()
+
+    def start(self):
+        pl.when(self.sends_right(1))(lambda: self.all_of(self.right[1], "start"))
+        pl.when(self.sends_left(1))(lambda: self.all_of(self.left[1], "start"))
+        self.all_of(self.own, "start")
+
+    def step(self, s):
+        def passed(got, over, onward, sends):
+            def run():
+                self.all_of(got[s], "wait_recv")
+                if s < self.steps:
+                    pl.when(sends(s + 1))(lambda: self.all_of(onward[s + 1], "start"))
+                self.all_of(over[s], "start")
+
+            return run
+
+        pl.when(self.gets_right(s))(
+            passed(self.right, self.over_right, self.right, self.sends_right)
+        )
+        pl.when(self.gets_left(s))(passed(self.left, self.over_left, self.left, self.sends_left))
+
+    def end(self):
+        self.all_of(self.own, "wait")
+        for s in range(1, self.steps + 1):
+            pl.when(self.gets_right(s))(lambda: self.all_of(self.over_right[s], "wait"))
+            pl.when(self.gets_left(s))(lambda: self.all_of(self.over_left[s], "wait"))
+
+    def drain(self):
+        for s in range(1, self.steps + 1):
+            pl.when(self.sends_right(s))(lambda: self.all_of(self.right[s], "wait_send"))
+            pl.when(self.sends_left(s))(lambda: self.all_of(self.left[s], "wait_send"))
+
+    @staticmethod
+    def remote(n, arrays):
+        return arrays * (1 + 4 * (n - 1))
+
+
+def back_kernel(
+    sizes,
+    partial, first, second, hidden_in, expert_in, cotangent, live, picks, router_t, router_low,
+    router_high, mixing, mixing_low, mixing_high, head_mix, mixing_lift, logs, gains, joined,
+    live_keys, tokens, own_in, own_lift, weights, attend_low, attend_high,
+    first_all, second_all, early_all, late_all, out_all, grad_all,
+    from_sibling, paired, received, second_got, early_got, late_got,
+    second_sum, early_sum, late_sum, early, late,
+    first_end, second_end, early_end, late_end,
+    first_mid, second_mid, early_mid, late_mid,
+    first_stage, second_stage, early_stage, late_stage,
+    first_final, second_final, early_final, late_final,
+    out_own, grad_own, grad_hidden, heads, stats, delta, heads_all, stats_all, grads,
+    send, recv, local,
 ):
+    place = Place(sizes)
+    wire = Wire(send, recv, local)
+    plane = place.dp_size * place.tp_size
+    me = place.dp * place.tp_size + place.tp
+    is_mid = jnp.logical_and(place.ctx >= 1, place.ctx <= 2)
+    is_end = jnp.logical_not(is_mid)
+    inner = lax.div(place.ctx, 2)
+    outer_half = 1 - inner
+    partner = jnp.where(is_mid, inner * 3, 1 + inner)
+    other_mid = 2 - inner
+    other_tp = lax.rem(place.tp + 1, 2)
     images, half = expert_in.shape[:2]
     count = images * half
-    start = pl.multiple_of(place[3], 16)
-    total = received[0].astype(F32)
-    for k in range(1, received.shape[0]):
-        total = total + received[k].astype(F32)
-    hidden = hidden_in[...]
-    layer_out[...] = (hidden + total[:, :D]).astype(BF16).reshape(images, half, D)
-    grad_probs = total[:, 2 * D : 2 * D + EXPERTS]
+    experts = first.shape[0]
+    start = pl.multiple_of(place.tp * half, 16)
+    own_start = pl.multiple_of(place.ctx * tokens.shape[1] + place.tp * half, 16)
+    critical = D + 128
+
+    barrier = pltpu.get_barrier_semaphore()
+    peers = []
+    for k in range(1, plane):
+        peer = lax.rem(me + k, plane)
+        peers.append((lax.div(peer, place.tp_size), lax.rem(peer, place.tp_size)))
+        pl.semaphore_signal(
+            barrier, inc=1, device_id={"dp": peers[-1][0], "tp": peers[-1][1]}, device_id_type=MESH
+        )
+    pl.semaphore_signal(barrier, inc=1, device_id={"ctx": partner}, device_id_type=MESH)
+
+    @pl.when(is_mid)
+    def _():
+        pl.semaphore_signal(barrier, inc=1, device_id={"ctx": other_mid}, device_id_type=MESH)
+
+    pl.semaphore_wait(barrier, plane + jnp.where(is_mid, 1, 0))
+
+    chunks = [
+        (
+            first.at[e], first_end.at[e], first_mid.at[e], first_stage.at[e],
+            first_final.at[e], functools.partial(lambda e, dp, tp: first_all.at[dp, tp, e], e),
+        )
+        for e in range(experts)
+    ]
+    chunks += [
+        (second_sum, second_end, second_mid, second_stage, second_final,
+         lambda dp, tp: second_all.at[dp, tp]),
+        (early_sum, early_end, early_mid, early_stage, early_final,
+         lambda dp, tp: early_all.at[dp, tp]),
+        (late_sum, late_end, late_mid, late_stage, late_final,
+         lambda dp, tp: late_all.at[dp, tp]),
+    ]
+    flows = []
+    for mine, end, mid, stage, final, slot in chunks:
+        flows.append(
+            dict(
+                outer=wire.copy(mine.at[outer_half], end.at[outer_half], {"ctx": partner}),
+                inner=wire.copy(mine.at[inner], end.at[inner], {"ctx": partner}),
+                cross=wire.copy(stage, mid, {"ctx": other_mid}),
+                back=wire.copy(final.at[inner], final.at[inner], {"ctx": partner}),
+                share=wire.copy(final.at[inner], final.at[inner], {"ctx": other_mid}),
+                pass_on=wire.copy(final.at[outer_half], final.at[outer_half], {"ctx": partner}),
+            )
+        )
+    late_waits = []
+
+    def send_end(k):
+        @pl.when(is_end)
+        def _():
+            flows[k]["outer"].start()
+            flows[k]["inner"].start()
+
+    def mid_first(k):
+        mine, end, mid, stage, final, slot = chunks[k]
+
+        @pl.when(is_mid)
+        def _():
+            flows[k]["outer"].wait_recv()
+            stage[...] = add_rounded(mine[outer_half], end[outer_half])
+            flows[k]["cross"].start()
+
+    def mid_second(k):
+        mine, end, mid, stage, final, slot = chunks[k]
+
+        @pl.when(is_mid)
+        def _():
+            flows[k]["inner"].wait_recv()
+            flows[k]["cross"].wait_recv()
+            final[inner] = add_rounded(mine[inner], end[inner], mid[...])
+            flows[k]["share"].start()
+            flows[k]["back"].start()
+
+    squared = place.chips == 2 and place.tp_size == 2
+    plane_flights, diagonals = {}, {}
+
+    def settle(k):
+        @pl.when(is_mid)
+        def _():
+            flows[k]["share"].wait_recv()
+            flows[k]["pass_on"].start()
+
+        @pl.when(is_end)
+        def _():
+            flows[k]["back"].wait_recv()
+            flows[k]["pass_on"].wait_recv()
+
+        final, slot = chunks[k][4], chunks[k][5]
+        spot = slot(place.dp, place.tp)
+        plane_flights[k] = []
+        for i, j in place.offsets():
+            if squared and i and j:
+                continue
+            dp, tp = place.ahead(i, j)
+            copy = wire.copy(final, spot, {"dp": dp, "tp": tp})
+            copy.start()
+            plane_flights[k].append((copy, i, j))
+        for copy in (wire.copy(final, spot, {"dp": place.sibling}), wire.near(final, spot)):
+            copy.start()
+            late_waits.append(copy)
+
+    def to_sibling(ref):
+        copy = wire.copy(ref, ref, {"dp": place.sibling})
+        copy.start()
+        late_waits.append(copy)
+
+    def forward(k):
+        slot = chunks[k][5]
+        for copy, i, j in sorted(plane_flights[k], key=lambda f: f[1]):
+            copy.wait_recv()
+            got = slot(*place.behind(i, j))
+            if squared and j:
+                dp, tp = place.ahead(1, 0)
+                diagonals[k] = wire.copy(got, got, {"dp": dp, "tp": tp})
+                diagonals[k].start()
+            to_sibling(got)
+
+    def diagonal(k):
+        if squared:
+            diagonals[k].wait_recv()
+            to_sibling(chunks[k][5](*place.behind(1, 1)))
+
+    stages = (mid_first, mid_second, settle, forward, diagonal)
+    reached = [0] * len(chunks)
+    SUM, FINAL, SENT, ONWARD, DONE = range(1, 6)
+
+    def go(k, stage):
+        while reached[k] < stage:
+            stages[reached[k]](k)
+            reached[k] += 1
+
+    def go_first(*pairs):
+        for k, stage in pairs:
+            if k < experts:
+                go(k, stage)
+
+    second_at, early_at, late_at = experts, experts + 1, experts + 2
+
+    def spread_start(values, got):
+        rows = got.shape[1]
+        copies = []
+        for k, (dp, tp) in enumerate(peers):
+            at = pl.ds(pl.multiple_of((dp * place.tp_size + tp) * rows, 16), rows)
+            copy = wire.copy(values.at[at], got.at[k], {"dp": dp, "tp": tp})
+            copy.start()
+            copies.append(copy)
+        return copies
+
+    def spread_end(copies, values, got, total):
+        rows = got.shape[1]
+        for copy in copies:
+            copy.wait()
+        added = values[pl.ds(pl.multiple_of(me * rows, 16), rows), :].astype(F32)
+        for k in range(plane - 1):
+            added = added + got[k].astype(F32)
+        total[...] = added.astype(BF16).reshape(total.shape)
+
+    swap = wire.copy(partial.at[1 - place.core], from_sibling, {"dp": place.sibling})
+    swap.start()
+    second_swap = wire.copy(second.at[other_tp], second_got, {"tp": other_tp})
+    second_swap.start()
+    for k in range(experts):
+        send_end(k)
+    swap.wait_recv()
+    returns = []
+    for lanes in (slice(0, critical), slice(critical, critical + D)):
+        copies = []
+        for i, j in place.offsets() + [(0, 0)]:
+            dp, tp = place.ahead(i, j)
+            chip = lax.div(dp, 2)
+            index = i * place.tp_size + j
+            if index:
+                paired[chip, tp, :, lanes] = add_rounded(
+                    partial[place.core, chip, tp, :, lanes], from_sibling[chip, tp, :, lanes]
+                )
+                copy = wire.copy(
+                    paired.at[chip, tp, :, lanes],
+                    received.at[index, :, lanes],
+                    {"dp": dp, "tp": tp},
+                )
+                copy.start()
+                copies.append(copy)
+            else:
+                received[0, :, lanes] = add_rounded(
+                    partial[place.core, chip, tp, :, lanes], from_sibling[chip, tp, :, lanes]
+                )
+        returns.append(copies)
+    late_sends = [swap] + returns[0] + returns[1]
+
+    go_first((0, SUM))
+    second_swap.wait()
+    second_sum[...] = add_rounded(second[place.tp], second_got[...])
+    send_end(second_at)
+    go_first((1, SUM), (0, FINAL), (2, SUM), (1, FINAL), (0, SENT))
+    for copy in returns[0]:
+        copy.wait_recv()
+
     own_sets = jnp.concatenate(
         [jnp.broadcast_to(picks[i : i + 1, :], (half, WIDTH)) for i in range(images)], axis=0
     )
-    grad_output = jnp.concatenate(
-        [cotangent[i, pl.ds(start, half), :] for i in range(images)], axis=0
+    total = received[0, :, :critical].astype(F32)
+    for k in range(1, received.shape[0]):
+        total = total + received[k, :, :critical].astype(F32)
+    hidden = hidden_in[...]
+    grad_probs = total[:, D : D + EXPERTS]
+    grad_output = (
+        jnp.concatenate([cotangent[i, pl.ds(start, half), :] for i in range(images)], axis=0)
     ).astype(F32) * live[...]
     rows = expert_in[...].reshape(count, D)
     router_lift = (times_transposed(rows, router_low[...]) * own_sets).astype(BF16)
@@ -987,189 +930,299 @@
     ).astype(BF16)
     grad_router_lift = (times_transposed(grad_logits, router_high[...]) * own_sets).astype(BF16)
     grad_expert_in = (
-        total[:, D : 2 * D]
+        total[:, :D]
         + matmul(grad_logits, router_t[...])
         + matmul(grad_router_lift, router_low[...])
     )
     _, unit, factor = normalize(hidden, gains[2:3, :], gains[3:4, :])
-    grad_hidden = grad_output + normalize_back(grad_expert_in, unit, factor, gains[2:3, :])
-    grad_hidden_out[...] = grad_hidden
-    grad_attended = grad_hidden.astype(BF16)
+    grad_rows = grad_output + normalize_back(grad_expert_in, unit, factor, gains[2:3, :])
+    grad_hidden[...] = grad_rows
+    grad_attended = grad_rows.astype(BF16)
     grad_mixing_lift = (times_transposed(grad_attended, mixing_high[...]) * own_sets).astype(BF16)
     grad_heads = (
         matmul(grad_attended, mixing[...]) + matmul(grad_mixing_lift, mixing_low[...])
     ).astype(BF16)
-    heads_out[...] = grad_heads.reshape(images, half, D)
+    heads[...] = grad_heads.reshape(images, half, D)
     mix = head_mix[...]
     lane = lax.broadcasted_iota(jnp.int32, (D, 128), 1)
     head = lax.div(lax.broadcasted_iota(jnp.int32, (D, 128), 0), HD)
     ones = (lane == head).astype(F32).astype(BF16)
-    delta = split_sum(grad_heads.astype(F32) * mix.astype(F32), ones)
-    delta_out[...] = delta
-    log = logs[...]
+    delta_rows = split_sum(grad_heads.astype(F32) * mix.astype(F32), ones)
+    delta[...] = delta_rows
+    log_rows = logs[...]
     for i in range(images):
         part = slice(i * half, (i + 1) * half)
         pad = jnp.zeros((128 - half, 128), F32)
-        stats = [jnp.concatenate([v[part], pad], axis=0).T[:HEADS] for v in (log, delta)]
+        turned = [
+            jnp.concatenate([v[part], pad], axis=0).T[:HEADS] for v in (log_rows, delta_rows)
+        ]
         row = 0
-        for rest, number in zip(stats, (3, 2)):
+        for rest, number in zip(turned, (3, 2)):
             for _ in range(number):
                 high = rest.astype(BF16)
-                stats_out[i, row : row + HEADS, :] = high
+                stats[i, row : row + HEADS, :] = high
                 rest = rest - high.astype(F32)
                 row += HEADS
-    products = (
-        inner_rows(grad_mixing_lift, mix),
-        inner_rows(mixing_lift[...], grad_attended),
-        inner_rows(grad_router_lift, rows),
-    )
-    tile = 0
-    for product in products:
-        for k in range(D // 128):
-            tiles[tile * WIDTH : (tile + 1) * WIDTH, :] = product[
-                :, k * 128 : (k + 1) * 128
-            ].astype(BF16)
-            tile += 1
+
+    def rows_slot(ctx, tp):
+        at = pl.multiple_of((ctx * place.tp_size + tp) * half, 16)
+        return heads_all.at[:, pl.ds(at, half), :]
+
+    chain = Chain(
+        place, wire, [heads, stats],
+        [rows_slot, lambda ctx, tp: stats_all.at[ctx * place.tp_size + tp]],
+    )
+    chain.start()
+
+    def put_tiles(target, products):
+        tile = 0
+        for product in products:
+            for n in range(product.shape[1] // 128):
+                target[tile * WIDTH : (tile + 1) * WIDTH, :] = product[
+                    :, n * 128 : (n + 1) * 128
+                ].astype(BF16)
+                tile += 1
+        if tile * WIDTH < target.shape[0]:
+            target[tile * WIDTH :, :] = jnp.zeros(
+                (target.shape[0] - tile * WIDTH, 128), BF16
+            )
+
     wide_logits = jnp.concatenate(
         [grad_logits, jnp.zeros((count, 128 - EXPERTS), BF16)], axis=1
     )
-    tiles[tile * WIDTH : (tile + 1) * WIDTH, :] = inner_rows(router_lift, wide_logits).astype(BF16)
-
-
-def middle(place, *operands):
-    images, half = operands[2].shape[:2]
-    count = images * half
-    tiles = 3 * (D // 128) + 1
-    return pl.pallas_call(
-        middle_kernel,
-        out_shape=(
-            jax.ShapeDtypeStruct((images, half, D), BF16),
-            jax.ShapeDtypeStruct((count, D), F32),
-            jax.ShapeDtypeStruct((images, half, D), BF16),
-            jax.ShapeDtypeStruct((images, 5 * HEADS, 128), BF16),
-            jax.ShapeDtypeStruct((count, 128), F32),
-            jax.ShapeDtypeStruct((tiles * WIDTH, 128), BF16),
+    put_tiles(
+        early,
+        (
+            inner_rows(grad_mixing_lift, mix),
+            inner_rows(mixing_lift[...], grad_attended),
+            inner_rows(grad_router_lift, rows),
+            inner_rows(router_lift, wide_logits),
         ),
-        in_specs=[pl.BlockSpec(memory_space=pltpu.SMEM)] + [IN_VMEM] * len(operands),
-        out_specs=(IN_VMEM,) * 6,
-        compiler_params=pltpu.CompilerParams(vmem_limit_bytes=48 << 20),
-    )(place, *operands)
-
-
-def attend_back_kernel(
-    place, joined, heads_all, stats_all, heads, logs, delta, live_keys, live_own, tokens, own_in,
-    own_lift, grad_hidden, weights, attend_low, attend_high, picks, gains, tiles_in,
-    tokens_grad, small, grads,
-):
-    images, seq = joined.shape[1:3]
-    half = heads.shape[1]
-    own_start = pl.multiple_of(place[0], 16)
-    start = pl.multiple_of(place[3], 16)
+    )
+    early_spread = spread_start(early, early_got)
+    go_first((3, SUM), (2, FINAL), (1, SENT))
+    chain.step(1)
+    go(second_at, SUM)
+    go_first((3, FINAL), (2, SENT))
+    chain.step(2)
+    go_first((0, ONWARD))
+    for s in range(3, chain.steps + 1):
+        chain.step(s)
+    spread_end(early_spread, early, early_got, early_sum)
+    send_end(early_at)
+    go(second_at, FINAL)
+    go_first((3, SENT))
+    chain.end()
+
     own = pl.ds(own_start, half)
     masks = half_masks()
     scale = HD**-0.5
-    blocks = seq // half
+
+    def heads_back(i, j):
+        part = slice(i * half, (i + 1) * half)
+        lanes = slice(j * 2 * HD, (j + 1) * 2 * HD)
+        open_keys = live_keys[i : i + 1, :] > 0
+        open_own = live[part] > 0
+        open_own = jnp.concatenate([open_own, open_own], axis=0)
+        found = jnp.concatenate(
+            [stats_all[n, i][:, :half].astype(F32) for n in range(stats_all.shape[0])], axis=1
+        )
+        log_t = found[0:HEADS] + found[HEADS : 2 * HEADS] + found[2 * HEADS : 3 * HEADS]
+        delta_t = found[3 * HEADS : 4 * HEADS] + found[4 * HEADS :]
+        q_all, k_all, v_all = (joined[p, i, :, lanes] for p in range(3))
+        g_all = heads_all[i, :, lanes]
+
+        def column(values):
+            return jnp.concatenate(
+                [values[:, 2 * j : 2 * j + 1], values[:, 2 * j + 1 : 2 * j + 2]], axis=0
+            )
+
+        def across(values):
+            return jnp.concatenate(
+                [
+                    jnp.broadcast_to(values[2 * j + n : 2 * j + n + 1, :], (half, values.shape[1]))
+                    for n in range(2)
+                ],
+                axis=0,
+            )
+
+        q = stack_pair(joined[0, i, own, lanes], masks, scale)
+        g = stack_pair(heads[i, :, lanes], masks)
+        scores = jnp.where(open_keys, times_transposed(q, k_all), MASKED)
+        probs = jnp.exp(scores - column(logs[part]))
+        grad_probs_att = times_transposed(g, v_all)
+        grad_scores = (probs * (grad_probs_att - column(delta[part]))).astype(BF16)
+        grads[0, part, lanes] = (join_pair(matmul(grad_scores, k_all), masks) * scale).astype(BF16)
+        k = stack_pair(joined[1, i, own, lanes], masks, scale)
+        v = stack_pair(joined[2, i, own, lanes], masks)
+        scores = jnp.where(open_own, times_transposed(k, q_all), MASKED)
+        probs = jnp.exp(scores - across(log_t))
+        grad_probs_att = times_transposed(v, g_all)
+        grad_scores = (probs * (grad_probs_att - across(delta_t))).astype(BF16)
+        grads[1, part, lanes] = (join_pair(matmul(grad_scores, q_all), masks) * scale).astype(BF16)
+        grads[2, part, lanes] = join_pair(matmul(probs.astype(BF16), g_all), masks).astype(BF16)
+
     for i in range(images):
-        part = slice(i * half, (i + 1) * half)
-        open_keys = live_keys[i : i + 1, :] > 0
-        open_own = live_own[part] > 0
-        open_own = jnp.concatenate([open_own, open_own], axis=0)
-        stats = jnp.concatenate(
-            [stats_all[n, i][:, :half].astype(F32) for n in range(blocks)], axis=1
-        )
-        log_t = stats[0:HEADS] + stats[HEADS : 2 * HEADS] + stats[2 * HEADS : 3 * HEADS]
-        delta_t = stats[3 * HEADS : 4 * HEADS] + stats[4 * HEADS :]
-        log_own, delta_own = logs[part], delta[part]
         for j in range(HEADS // 2):
-            lanes = slice(j * 2 * HD, (j + 1) * 2 * HD)
-            q_all, k_all, v_all = (joined[p, i, :, lanes] for p in range(3))
-            g_all = heads_all[i, :, lanes]
-
-            def column(values):
-                return jnp.concatenate(
-                    [values[:, 2 * j : 2 * j + 1], values[:, 2 * j + 1 : 2 * j + 2]], axis=0
-                )
-
-            def row(values):
-                return jnp.concatenate(
-                    [
-                        jnp.broadcast_to(values[2 * j + n : 2 * j + n + 1, :], (half, seq))
-                        for n in range(2)
-                    ],
-                    axis=0,
-                )
-
-            q = stack_pair(joined[0, i, own, lanes], masks, scale)
-            g = stack_pair(heads[i, :, lanes], masks)
-            scores = jnp.where(open_keys, times_transposed(q, k_all), MASKED)
-            probs = jnp.exp(scores - column(log_own))
-            grad_probs = times_transposed(g, v_all)
-            grad_scores = (probs * (grad_probs - column(delta_own))).astype(BF16)
-            grads[0, part, lanes] = (
-                join_pair(matmul(grad_scores, k_all), masks) * scale
-            ).astype(BF16)
-            k = stack_pair(joined[1, i, own, lanes], masks, scale)
-            v = stack_pair(joined[2, i, own, lanes], masks)
-            scores = jnp.where(open_own, times_transposed(k, q_all), MASKED)
-            probs = jnp.exp(scores - row(log_t))
-            grad_probs = times_transposed(v, g_all)
-            grad_scores = (probs * (grad_probs - row(delta_t))).astype(BF16)
-            grads[1, part, lanes] = (
-                join_pair(matmul(grad_scores, q_all), masks) * scale
-            ).astype(BF16)
-            grads[2, part, lanes] = join_pair(matmul(probs.astype(BF16), g_all), masks).astype(
-                BF16
-            )
-    own_sets = jnp.concatenate(
-        [jnp.broadcast_to(picks[i : i + 1, :], (half, WIDTH)) for i in range(images)], axis=0
-    )
+            heads_back(i, j)
+        if i == 0:
+            go(early_at, SUM)
+            go(second_at, SENT)
+            go_first((1, ONWARD), (2, ONWARD), (0, DONE))
+    go(early_at, FINAL)
     lift = times_transposed(grads[0], attend_high[0])
     into = times_transposed(grads[0], weights[0])
     for p in range(1, 3):
         lift = lift + times_transposed(grads[p], attend_high[p])
         into = into + times_transposed(grads[p], weights[p])
     lift = (lift * own_sets).astype(BF16)
+    lift_in = own_lift[...].reshape(count, WIDTH)
+    put_tiles(
+        late,
+        [inner_rows(lift_in, grads[p]) for p in range(3)]
+        + [inner_rows(lift, own_in[...].reshape(count, D))],
+    )
+    late_spread = spread_start(late, late_got)
     into = into + matmul(lift, attend_low[...])
     flat = jnp.concatenate(
         [tokens[i, pl.ds(start, half), :] for i in range(images)], axis=0
     ).astype(F32)
     _, unit, factor = normalize(flat, gains[0:1, :], gains[1:2, :])
     result = grad_hidden[...] + normalize_back(into, unit, factor, gains[0:1, :])
-    tokens_grad[...] = result.astype(BF16).reshape(images, half, D)
-    rows_in = own_in[...].reshape(images * half, D)
-    lift_in = own_lift[...].reshape(images * half, WIDTH)
-    products = [inner_rows(lift_in, grads[p]) for p in range(3)] + [inner_rows(lift, rows_in)]
-    tile = 0
-    for product in products:
-        for n in range(D // 128):
-            small[tile * WIDTH : (tile + 1) * WIDTH, :] = product[
-                :, n * 128 : (n + 1) * 128
-            ].astype(BF16)
-            tile += 1
-    done = tile * WIDTH + tiles_in.shape[0]
-    small[tile * WIDTH : done, :] = tiles_in[...]
-    if done < small.shape[0]:
-        small[done:, :] = jnp.zeros((small.shape[0] - done, 128), BF16)
-
-
-def attend_back(small_rows, place, *operands):
-    images, half = operands[3].shape[:2]
-    count = images * half
+    grad_own[...] = result.astype(BF16).reshape(images, half, D)
+    for copy in returns[1]:
+        copy.wait_recv()
+    total = hidden_in[...]
+    for k in range(received.shape[0]):
+        total = total + received[k, :, critical:].astype(F32)
+    out_own[...] = total.astype(BF16).reshape(images, half, D)
+    for values, gathered in ((out_own, out_all), (grad_own, grad_all)):
+        spot = gathered.at[:, pl.ds(start, half), :]
+        for copy in (wire.copy(values, spot, {"tp": other_tp}), wire.near(values, spot)):
+            copy.start()
+            late_waits.append(copy)
+    spread_end(late_spread, late, late_got, late_sum)
+    send_end(late_at)
+    go(early_at, SENT)
+    go_first((1, DONE), (3, ONWARD))
+    go(late_at, SUM)
+    go_first((2, DONE))
+    go(second_at, ONWARD)
+    go(late_at, FINAL)
+    go_first((3, DONE))
+    go(late_at, SENT)
+    go(early_at, ONWARD)
+    go(second_at, DONE)
+    go(late_at, ONWARD)
+    for k in range(len(chunks)):
+        go(k, DONE)
+
+    @pl.when(is_end)
+    def _():
+        for flow in flows:
+            flow["outer"].wait_send()
+            flow["inner"].wait_send()
+
+    @pl.when(is_mid)
+    def _():
+        for flow in flows:
+            for name in ("cross", "back", "share", "pass_on"):
+                flow[name].wait_send()
+
+    chain.drain()
+    for copy in late_sends:
+        copy.wait_send()
+    for k in plane_flights:
+        for copy, _, _ in plane_flights[k]:
+            copy.wait_send()
+    for k in diagonals:
+        diagonals[k].wait_send()
+    for copy in late_waits:
+        copy.wait()
+
+
+def back(sizes, partial, first, second, *operands):
+    dp, ctx, tp = sizes
+    assert ctx == 4 and tp == 2
+    experts, _, width, lanes = first.shape
+    part = second.shape[1:]
+    plane = dp * tp
+    chips = dp // 2
+    count, sent = partial.shape[3:]
+    images = operands[1].shape[0]
+    half = count // images
+    seq = ctx * tp * half
+
+    def small_rows(tiles):
+        return -(-tiles * WIDTH // (plane * 16)) * 16
+
+    early_rows, late_rows = small_rows(3 * (D // 128) + 1), small_rows(4 * (D // 128))
+    small = [(2, rows // 2, 128) for rows in (early_rows, late_rows)]
+    chunks = experts + 3
+    offsets = place_offsets(sizes, True)
+    remote = (
+        chunks * (6 + 2 * offsets + 1)
+        + 2
+        + 2 * offsets
+        + 2 * (plane - 1)
+        + Chain.remote(ctx, 2)
+        + 2
+    )
+
+    def vmem(*shape, dtype=BF16):
+        return pltpu.VMEM(shape, dtype)
+
+    shapes = [(experts, 2, width, lanes), part] + small
+    halves = [(experts, width, lanes)] + [shape[1:] for shape in shapes[1:]]
     return pl.pallas_call(
-        attend_back_kernel,
+        functools.partial(back_kernel, sizes),
         out_shape=(
-            jax.ShapeDtypeStruct((images, half, D), BF16),
-            jax.ShapeDtypeStruct((small_rows, 128), BF16),
+            jax.ShapeDtypeStruct((dp, tp) + first.shape, BF16),
+            jax.ShapeDtypeStruct((dp, tp) + part, BF16),
+            jax.ShapeDtypeStruct((dp, tp) + small[0], BF16),
+            jax.ShapeDtypeStruct((dp, tp) + small[1], BF16),
+            jax.ShapeDtypeStruct((images, tp * half, D), BF16),
+            jax.ShapeDtypeStruct((images, tp * half, D), BF16),
         ),
-        in_specs=[pl.BlockSpec(memory_space=pltpu.SMEM)] + [IN_VMEM] * len(operands),
-        out_specs=(IN_VMEM,) * 2,
-        scratch_shapes=[pltpu.VMEM((3, count, D), BF16)],
-        compiler_params=pltpu.CompilerParams(vmem_limit_bytes=48 << 20),
-    )(place, *operands)
+        in_specs=[IN_VMEM] * (3 + len(operands)),
+        out_specs=(ANY,) * 6,
+        scratch_shapes=[
+            vmem(chips, tp, count, sent),
+            vmem(chips, tp, count, sent),
+            vmem(chips * tp, count, sent),
+            vmem(*part),
+            vmem(plane - 1, early_rows, 128),
+            vmem(plane - 1, late_rows, 128),
+            vmem(*part),
+            vmem(*small[0]),
+            vmem(*small[1]),
+            vmem(plane * early_rows, 128),
+            vmem(plane * late_rows, 128),
+        ]
+        + [vmem(*shape) for shape in shapes]
+        + [vmem(*shape) for shape in halves]
+        + [vmem(*shape) for shape in halves]
+        + [vmem(*shape) for shape in shapes]
+        + [
+            vmem(images, half, D),
+            vmem(images, half, D),
+            vmem(count, D, dtype=F32),
+            vmem(images, half, D),
+            vmem(images, 5 * HEADS, 128),
+            vmem(count, 128, dtype=F32),
+            vmem(images, seq, D),
+            vmem(ctx * tp, images, 5 * HEADS, 128),
+            vmem(3, count, D),
+        ]
+        + semaphores(remote, chunks + 2 + 2),
+        compiler_params=pltpu.CompilerParams(
+            collective_id=3, has_side_effects=True, vmem_limit_bytes=56 << 20
+        ),
+    )(partial, first, second, *operands)
 
 
 def assemble_kernel(
-    first, second, small, up, down_t, narrow_t, narrow,
+    first, second, early, late, up, down_t, narrow_t, narrow,
     attend_down, attend_up, mixing_down, mixing_up, router_down, router_up,
 ):
     lanes, part = first.shape[-1], second.shape[-1]
@@ -1185,20 +1238,22 @@
 
     @pl.when(pl.program_id(0) == 0)
     def _():
-        def tile(k):
+        def tile(small, k):
             return small[k * WIDTH : (k + 1) * WIDTH, :].astype(F32).reshape(SETS, RANK, 128)
 
         count = D // 128
         for p in range(3):
             for k in range(count):
-                attend_up[:, p, :, k * 128 : (k + 1) * 128] = tile(p * count + k)
-        for p, out in enumerate((attend_down, mixing_down, mixing_up, router_down)):
+                attend_up[:, p, :, k * 128 : (k + 1) * 128] = tile(late, p * count + k)
+        for k in range(count):
+            attend_down[:, :, k * 128 : (k + 1) * 128] = tile(late, 3 * count + k)
+        for p, out in enumerate((mixing_down, mixing_up, router_down)):
             for k in range(count):
-                out[:, :, k * 128 : (k + 1) * 128] = tile((p + 3) * count + k)
-        router_up[...] = tile(7 * count)[:, :, :EXPERTS]
-
-
-def assemble(first, second, small):
+                out[:, :, k * 128 : (k + 1) * 128] = tile(early, p * count + k)
+        router_up[...] = tile(early, 3 * count)[:, :, :EXPERTS]
+
+
+def assemble(first, second, early, late):
     dp, tp, experts, _, width, lanes = first.shape
     part = second.shape[-1]
 
@@ -1235,11 +1290,12 @@
             pl.BlockSpec(
                 (1, tp, 2, 1, width, part), lambda e: (split(e)[0], 0, 0, split(e)[1], 0, 0)
             ),
-            pl.BlockSpec(small.shape, lambda e: (0, 0)),
+            pl.BlockSpec(early.shape, lambda e: (0, 0)),
+            pl.BlockSpec(late.shape, lambda e: (0, 0)),
         ],
         out_specs=[out[1] for out in outs],
         compiler_params=pltpu.CompilerParams(vmem_limit_bytes=32 << 20),
-    )(first, second, small)
+    )(first, second, early, late)
 
 
 def per_device(
@@ -1272,7 +1328,6 @@
     shrink_up,
 ):
     dp_size, ctx_size, tp_size = sizes
-    plane = dp_size * tp_size
     images, block = tokens.shape[:2]
     half = block // tp_size
     count = images * half
@@ -1342,25 +1397,16 @@
         jnp.transpose(shrink_down, (0, 1, 3, 2)),
         shrink_up,
     )
-    received = return_rows(
-        sizes, partial.reshape(2, dp_size // 2, tp_size, count, partial.shape[-1])
-    )
-    layer_out, grad_hidden, heads, stats, delta, tiles = middle(
-        place, received, hidden, expert_in, cotangent, own_live, own_picks, router_t, router_low,
-        router_high, mixing_all, mixing_low, mixing_high, head_mix, mixing_lift, logs, gains,
-    )
-    heads_all, stats_all = heads_gather(sizes, heads, stats)
-    needed = (7 * (D // 128) + 1) * WIDTH
-    rows = -(-needed // (plane * 16)) * 16
-    tokens_grad, small = attend_back(
-        plane * rows, place, joined, heads_all, stats_all, heads, logs, delta, key_live, own_live,
-        tokens, own_in, own_lift, grad_hidden, weights_all, attend_low, attend_high, own_picks,
-        gains, tiles,
-    )
-    first_all, second_all, small_all, out_all, grad_all = finish(
-        sizes, first_grads, second_grads, small.reshape(plane, rows, 128), layer_out, tokens_grad
-    )
-    wide = assemble(first_all, second_all, small_all.reshape(plane * rows, 128))
+    first_all, second_all, early_all, late_all, out_all, grad_all = back(
+        sizes,
+        partial.reshape(2, dp_size // 2, tp_size, count, partial.shape[-1]),
+        first_grads, second_grads, hidden, expert_in, cotangent, own_live, own_picks, router_t,
+        router_low, router_high, mixing_all, mixing_low, mixing_high, head_mix, mixing_lift, logs,
+        gains, joined, key_live, tokens, own_in, own_lift, weights_all, attend_low, attend_high,
+    )
+    wide = assemble(
+        first_all, second_all, early_all.reshape(-1, 128), late_all.reshape(-1, 128)
+    )
 
     def flipped(values):
         return jnp.swapaxes(values, -1, -2)

time: 265 us -> 235 us (0.89)
  Pallas kernels: 236 us -> 200 us
  local copies, waits for them, and re-layouts: 22.2 us -> 28.5 us
    pallas_call x5 -> x1, Pallas kernels: 148 us -> 113 us  [back(): pl.pallas_call(functools.partial(back_kernel, sizes), out_shape=(jax.Shap...]
    unnamed x57 -> x69, local copies, waits for them, and re-layouts: 18.1 us -> 23.7 us
where the time goes in v1:
time: 235 us
  Pallas kernels  200 us (85%)
  local copies, waits for them, and re-layouts  28.5 us (12%)
  other arithmetic  4.82 us (2%)
    pallas_call x1, Pallas kernels, back(): pl.pallas_call(functools.partial(back_kernel, sizes), out_shape=(jax.Shap...  113 us
    pallas_call x1, Pallas kernels, start_gather(): pl.pallas_call(functools.partial(start_kernel, sizes), out_shape=(jax.Sha...  27.9 us
    pallas_call x1, Pallas kernels, run_experts(): pl.pallas_call(experts_kernel, grid_spec=pltpu.PrefetchScalarGridSpec(num...  25 us
    unnamed x69, local copies, waits for them, and re-layouts  23.7 us
    pallas_call x1, Pallas kernels, expert_in_gather(): pl.pallas_call(functools.partial(expert_in_kernel, sizes), out_shape=jax....  12.5 us
    pallas_call x1, Pallas kernels, attend(): pl.pallas_call(attend_kernel, out_shape=(out(3, images, seq, D), out(imag...  12.2 us
    pallas_call x1, Pallas kernels, assemble(): pl.pallas_call(assemble_kernel, grid=(EXPERTS,), out_shape=[out[0] for ou...  10.1 us

profile of v1, /device:TPU:1, one launch (start us, length us, event | category | flops | bytes accessed | tf_op | source)
XLA Modules:
  0.0 234.6 jit_solution(11163968560422386057)
XLA Ops:
  0.7 0.1 pad_add_fusion.1.place
  0.7 0.0 copy-start.29
  0.7 0.7 compare_convert_fusion.2.picks
  1.5 0.0 copy-start.28
  1.5 0.8 broadcast_multiply_fusion
  2.2 0.1 dynamic-slice_convert_fusion
  2.3 1.4 copy.51.router_high_t
  3.7 0.7 pad_maximum_fusion.gains
  4.4 0.0 copy-start.23
  4.4 0.7 broadcast_in_dim.5
  5.2 0.7 pad_add_fusion.ints
  5.9 0.8 convert_element_type.18.live
  6.7 0.9 copy.48
  7.6 0.0 copy-start.5
  7.6 0.0 copy-start.7
  7.6 1.0 copy-done.7
  8.7 1.0 copy-done.8
  9.6 0.9 copy-done.18
  10.6 0.8 copy-done.24
  11.4 0.7 copy-done.30
  12.1 27.9 %shard_map.337 = (bf16[2,640,512]{2,1,0:T(8,128)(2,1)S(1)}, bf16[3,512,512]{2,1,0:T(8,128)(2,1)S(1)}, bf16[512,512]{1,0:T(8,128)(2,1)S(1)}, bf16[4,16,128]{2,1,0...) custom-call(bf16[2,160,512]{2,1,0:T(8,128)(2,1)S(1)} %copy-done.7, ...), custom_call_target="tpu_custom_call" | custom-call | tf_op jit(solution)/shard_map/pallas_call | solution.py:270
  40.0 0.0 copy-start.6
  40.0 1.1 copy-done.6
  41.1 1.1 copy-done.9
  42.2 0.2 slice_reduce_fusion
  42.4 0.9 compare_convert_fusion.1.picks
  43.4 0.1 reshape.161.live_keys
  43.5 0.6 copy_bitcast_fusion.router_t
  44.1 0.8 compare_convert_fusion.picks_t
  44.9 1.3 copy-done.10
  46.2 0.8 copy-done.13
  47.0 0.8 copy-done.14
  47.9 0.8 copy-done.15
  48.7 12.2 %shard_map.338 = (bf16[3,2,640,512]{3,2,1,0:T(8,128)(2,1)}, bf16[2,80,512]{2,1,0:T(8,128)(2,1)S(1)}, bf16[2,80,64]{2,1,0:T(8,128)(2,1)S(1)}, bf16[160,512]{1,0:T...) custom-call(s32[4]{0:T(128)S(1)} %pad_add_fusion.1.place, ...), custom_call_target="tpu_custom_call" | custom-call | tf_op jit(solution)/shard_map/pallas_call | solution.py:407
  60.9 0.7 copy-done.12
  61.6 0.6 copy-done.19
  62.3 0.7 copy-done.20
  62.9 0.6 copy-done.21
  63.6 0.6 copy-done.26
  64.2 0.6 copy-done.27
  64.8 12.5 %shard_map.339.rows_all = bf16[8,160,512]{2,1,0:T(8,128)(2,1)S(1)} custom-call(bf16[2,80,512]{2,1,0:T(8,128)(2,1)S(1)} %get-tuple-element.50.own.expert_in), custom_call_target="tpu_custom_call" | custom-call | tf_op jit(solution)/shard_map/pallas_call | solution.py:304
  77.3 0.0 copy-done.29
  77.3 0.0 copy-done.22
  77.3 0.0 copy-start.2
  77.3 1.0 copy-done.2
  78.4 25.0 %shard_map.340 = (bf16[4,2,64,1024]{3,2,1,0:T(8,128)(2,1)}, bf16[2,2,4,64,256]{4,3,2,1,0:T(8,128)(2,1)}, bf16[2,2,2,2,80,1152]{5,4,3,2,1,0:T(8,128)(2,1)}) custom-call(s32[4]{0:T(128)} %copy-done.29, bf16[8,160,512]{2,1,0:T(8,128)(2,1)} %copy-done.2, bf16[8,160,512]{2,1,0:T(8,128)(2,1)} %copy-done.6, s32[8,8,160]{2,1,0:T(8,128)} %copy-done.22, ...), custom_call_target="tpu_custom_call" | custom-call | tf_op jit(solution)/shard_map/pallas_call | solution.py:554
  103.4 0.0 copy-done.28
  103.4 0.0 copy-done.23
  103.4 0.0 copy-done.5
  103.4 0.0 copy-done.1
  103.5 0.0 copy-done.3
  103.5 0.0 copy-done.25
  103.5 0.0 copy-done.11
  103.5 112.7 %shard_map.341 = (bf16[4,2,4,2,64,1024]{5,4,3,2,1,0:T(8,128)(2,1)}, bf16[4,2,2,4,64,256]{5,4,3,2,1,0:T(8,128)(2,1)}, bf16[4,2,2,56,128]{4,3,2,1,0:T(8,128)(2,1)}...) custom-call(bf16[2,2,2,160,1152]{4,3,2,1,0:T(8,128)(2,1)} %bitcast.62, ...), custom_call_target="tpu_custom_call" | custom-call | tf_op jit(solution)/shard_map/pallas_call | solution.py:1177
  216.1 0.0 copy-start
  216.2 3.4 %copy-done = bf16[4,2,4,2,64,1024]{5,4,3,2,1,0:T(8,128)(2,1)S(1)} copy-done((bf16[4,2,4,2,64,1024]{5,4,3,2,1,0:T(8,128)(2,1)S(1)}, bf16[4,2,4,2,64,1024]{5,4,3,2,1,0:T(8,128)(2,1)}, u32[]{:S(2)}) %copy-start) | copy-done | bytes 8388632
  219.5 1.6 copy-done.4
  221.1 0.9 copy-done.16
  222.1 0.9 copy-done.17
  223.0 10.1 %shard_map.342 = (f32[4,16,16,2048]{3,2,1,0:T(8,128)}, f32[4,16,16,2048]{3,2,1,0:T(8,128)}, f32[4,16,16,512]{3,2,1,0:T(8,128)}, f32[4,16,16,512]{3,2,1,0:T(8,128...) custom-call(bf16[4,2,4,2,64,1024]{5,4,3,2,1,0:T(8,128)(2,1)S(1)} %co, ...), custom_call_target="tpu_custom_call" | custom-call | tf_op jit(solution)/shard_map/pallas_call | solution.py:1282
  233.1 0.0 copy-done.32
  233.1 0.7 copy.60
  233.8 0.0 copy-done.31
  233.8 0.7 copy.61
  (30 shorter events, 0.1 us)
Async XLA Ops:
  0.7 76.6 %copy-start.29 = (s32[4]{0:T(128)}, s32[4]{0:T(128)S(1)}, u32[]{:S(2)}) copy-start(s32[4]{0:T(128)S(1)} %pad_add_fusion.1.place) | copy-start | bytes 52
  1.5 102.0 %copy-start.28 = (f32[2,64]{1,0:T(2,128)}, f32[2,64]{1,0:T(2,128)S(1)}, u32[]{:S(2)}) copy-start(f32[2,64]{1,0:T(2,128)S(1)} %compare_convert_fusion.2.picks) | copy-start | bytes 1540
  4.4 99.0 %copy-start.23 = (f32[4,512]{1,0:T(4,128)}, f32[4,512]{1,0:T(4,128)S(1)}, u32[]{:S(2)}) copy-start(f32[4,512]{1,0:T(4,128)S(1)} %pad_maximum_fusion.gains) | copy-start | bytes 24580
  7.6 95.8 %copy-start.5 = (bf16[3,4,16,512]{3,2,1,0:T(8,128)(2,1)}, bf16[3,4,16,512]{3,2,1,0:T(8,128)(2,1)S(1)}, u32[]{:S(2)}) copy-start(bf16[3,4,16,512]{3,2,1,0:T(8,128)(2,1)S(1)} %copy.48) | copy-start | bytes 589828
  7.6 1.0 copy-start.7
  8.7 1.0 copy-start.8
  9.6 0.9 copy-start.18
  10.6 0.8 copy-start.24
  11.4 0.7 copy-start.30
  40.0 1.1 copy-start.6
  41.1 1.1 copy-start.9
  42.2 35.1 %copy-start.22 = (s32[8,8,160]{2,1,0:T(8,128)}, s32[8,8,160]{2,1,0:T(8,128)S(1)}, u32[]{:S(2)}) copy-start(s32[8,8,160]{2,1,0:T(8,128)S(1)} %get-tuple-element.52.ints) | copy-start | bytes 122884
  42.2 61.3 %copy-start.1 = (bf16[3,512,512]{2,1,0:T(8,128)(2,1)}, bf16[3,512,512]{2,1,0:T(8,128)(2,1)S(1)}, u32[]{:S(2)}) copy-start(bf16[3,512,512]{2,1,0:T(8,128)(2,1)S(1)} %get-tuple-element.47.weights) | copy-start | bytes 4718596
  42.2 61.3 %copy-start.3 = (bf16[512,512]{1,0:T(8,128)(2,1)}, bf16[512,512]{1,0:T(8,128)(2,1)S(1)}, u32[]{:S(2)}) copy-start(bf16[512,512]{1,0:T(8,128)(2,1)S(1)} %get-tuple-element.48.mixing) | copy-start | bytes 1572868
  43.5 60.0 %copy-start.25 = (s32[2,640]{1,0:T(2,128)}, s32[2,640]{1,0:T(2,128)S(1)}, u32[]{:S(2)}) copy-start(s32[2,640]{1,0:T(2,128)S(1)} %reshape.161.live_keys) | copy-start | bytes 15364
  44.9 1.3 copy-start.10
  46.2 0.8 copy-start.13
  47.0 0.8 copy-start.14
  47.9 0.8 copy-start.15
  60.9 0.7 copy-start.12
  61.6 0.7 copy-start.19
  62.3 0.7 copy-start.20
  62.9 0.6 copy-start.21
  63.6 0.6 copy-start.26
  64.2 0.6 copy-start.27
  64.8 38.7 %copy-start.11 = (bf16[2,80,512]{2,1,0:T(8,128)(2,1)}, bf16[2,80,512]{2,1,0:T(8,128)(2,1)S(1)}, u32[]{:S(2)}) copy-start(bf16[2,80,512]{2,1,0:T(8,128)(2,1)S(1)} %get-tuple-element.50.own.expert_in) | copy-start | bytes 491524
  77.3 1.1 copy-start.2
  216.1 3.4 %copy-start = (bf16[4,2,4,2,64,1024]{5,4,3,2,1,0:T(8,128)(2,1)S(1)}, bf16[4,2,4,2,64,1024]{5,4,3,2,1,0:T(8,128)(2,1)}, u32[]{:S(2)}) copy-start(bf16[4,2,4,2,64,1024]{5,4,3,2,1,0:T(8,128)(2,1)} %get-tuple-element.66.first) | copy-start | bytes 25165828
  219.5 1.6 copy-start.4
  221.1 0.9 copy-start.16
  222.1 0.9 copy-start.17
  223.0 10.1 %copy-start.32 = (bf16[2,160,512]{2,1,0:T(8,128)(2,1)S(1)}, bf16[2,160,512]{2,1,0:T(8,128)(2,1)}, u32[]{:S(2)}) copy-start(bf16[2,160,512]{2,1,0:T(8,128)(2,1)} %get-tuple-element.92) | copy-start | bytes 983044
  223.0 10.8 %copy-start.31 = (bf16[2,160,512]{2,1,0:T(8,128)(2,1)S(1)}, bf16[2,160,512]{2,1,0:T(8,128)(2,1)}, u32[]{:S(2)}) copy-start(bf16[2,160,512]{2,1,0:T(8,128)(2,1)} %get-tuple-element.93) | copy-start | bytes 983044
